TPU v7x, 32 devices: a whole 2x2x4 slice. The times are simulated.
32 devices in a mesh: rep: 4 (over y, x), fsdp: 4 (over z), ctx: 2 (over core).
Axes of the slice: x: 2, y: 2, z: 4, core: 2. Of those that a mesh axis runs over, the one named last changes fastest.
Arguments:
- inputs: bfloat16 [2, 16, 1024, 768], P(None, ('rep', 'fsdp'), 'ctx'), may hold values from -6 to 6
- weight_qkv: bfloat16 [768, 2304], P('fsdp'), may hold values from -0.21875 to 0.21875
- bias_query: bfloat16 [768], P('fsdp'), may hold values from -3 to 3
- bias_value: bfloat16 [768], P('fsdp'), may hold values from -3 to 3
- weight_mix: bfloat16 [768, 768], P('fsdp'), may hold values from -1.75 to 1.75
- bias_mix: bfloat16 [768], P('fsdp'), may hold values from -2 to 2
- gain_attn: bfloat16 [768], P('fsdp'), may hold values from 0.099609375 to 1.8984375
- shift_attn: bfloat16 [768], P('fsdp'), may hold values from -2 to 2
- gain_mlp: bfloat16 [768], P('fsdp'), may hold values from 0.099609375 to 1.8984375
- shift_mlp: bfloat16 [768], P('fsdp'), may hold values from -2 to 2
- weight_up: bfloat16 [768, 3072], P('fsdp'), may hold values from -0.21875 to 0.21875
- bias_up: bfloat16 [3072], P('fsdp'), may hold values from -3 to 3
- weight_down: bfloat16 [3072, 768], P('fsdp'), may hold values from -0.109375 to 0.109375
- bias_down: bfloat16 [768], P('fsdp'), may hold values from -2 to 2
- cotangent: bfloat16 [2, 16, 1024, 768], P(None, ('rep', 'fsdp'), 'ctx'), may hold values from -6 to 6
Outputs:
- outputs: bfloat16 [2, 16, 1024, 768], P(None, ('rep', 'fsdp'), 'ctx')
- grad_inputs: float32 [2, 16, 1024, 768], P(None, ('rep', 'fsdp'), 'ctx')
- weight_qkv_grad: float32 [768, 2304], P('fsdp')
- bias_query_grad: float32 [768], P('fsdp')
- bias_value_grad: float32 [768], P('fsdp')
- weight_mix_grad: float32 [768, 768], P('fsdp')
- bias_mix_grad: float32 [768], P('fsdp')
- gain_attn_grad: float32 [768], P('fsdp')
- shift_attn_grad: float32 [768], P('fsdp')
- gain_mlp_grad: float32 [768], P('fsdp')
- shift_mlp_grad: float32 [768], P('fsdp')
- weight_up_grad: float32 [768, 3072], P('fsdp')
- bias_up_grad: float32 [3072], P('fsdp')
- weight_down_grad: float32 [3072, 768], P('fsdp')
- bias_down_grad: float32 [768], P('fsdp')
All inputs are finite; a program needn't handle non-finite values.
Results may differ from a plain program's by a relative error of at most 0.018.
Values may be sent and summed in bfloat16 or wider, within the bound.
A program may use at most 320 MiB of HBM per device.

v0:
```python
from functools import partial

import jax
import jax.numpy as jnp
from jax import lax
from jax.experimental import pallas as pl
from jax.experimental.pallas import tpu as pltpu
from jax.sharding import PartitionSpec as P

H = 12
EPS = 1e-05
BF16 = jnp.bfloat16
F32 = jnp.float32
QB = 256
TB = 256
FP = 256
SHARES = 4
GELU_A = 0.7978845608028654
GELU_B = 0.044715
LOG2E = 1.4426950408889634


def norm_stats(values):
    center = values - jnp.mean(values, axis=-1, keepdims=True)
    inverse = lax.rsqrt(jnp.mean(center * center, axis=-1, keepdims=True) + EPS)
    return (center * inverse, inverse)


def norm_back(grad_norm, normal, inverse, gain):
    scaled = grad_norm * gain
    return inverse * (
        scaled
        - jnp.mean(scaled, axis=-1, keepdims=True)
        - normal * jnp.mean(scaled * normal, axis=-1, keepdims=True)
    )


def outer_sum(left, right):
    return jnp.einsum("sri,srj->ij", left, right, preferred_element_type=F32)


def project(left, weight):
    return jnp.einsum("sri,ij->srj", left, weight, preferred_element_type=F32)


def project_back(grad_rows, weight):
    return jnp.einsum("srj,ij->sri", grad_rows, weight, preferred_element_type=F32)


def dot_nt(a, b):
    return lax.dot_general(a, b, (((1,), (1,)), ((), ())), preferred_element_type=F32)


def dot_nn(a, b):
    return lax.dot_general(a, b, (((1,), (0,)), ((), ())), preferred_element_type=F32)


def head_mask(x, head, size):
    lane = lax.broadcasted_iota(jnp.int32, x.shape, 1)
    keep = (lane >= head * size) & (lane < (head + 1) * size)
    return jnp.where(keep, x, jnp.zeros_like(x))


def causal(scores_t, qb):
    n = scores_t.shape[0]
    bottom = scores_t[n - QB :]
    key = lax.broadcasted_iota(jnp.int32, bottom.shape, 0)
    query = lax.broadcasted_iota(jnp.int32, bottom.shape, 1)
    bottom = jnp.where(key <= query, bottom, -1e30)
    return bottom if n == QB else jnp.concatenate([scores_t[: n - QB], bottom], axis=0)


def attention_forward_kernel(factor, size, q_ref, k_ref, v_ref, o_ref, lse_ref):
    refs = [ref.at[0] for ref in (q_ref, k_ref, v_ref, o_ref)]
    attention_forward_block(factor, size, *refs, lse_ref.at[0, 0], lambda done: None)


def attention_forward_block(factor, size, q_ref, k_ref, v_ref, o_ref, lse_ref, between):
    length = q_ref.shape[0]
    base_two = factor * LOG2E
    k = k_ref[...]
    vt = jnp.transpose(v_ref[...])
    for qb in range(length // QB):
        n = (qb + 1) * QB
        rows = pl.ds(qb * QB, QB)
        q = q_ref[rows, :]
        outs = []
        for head in range(2):
            s = causal(dot_nt(k[:n], head_mask(q, head, size)), qb)
            top = jnp.max(s, axis=0, keepdims=True) * base_two
            p = jnp.exp2(s * base_two - top)
            total = jnp.sum(p, axis=0, keepdims=True)
            o = dot_nn(vt[head * size : (head + 1) * size, :n], p.astype(BF16))
            outs.append(o * (1.0 / total))
            lse_ref[head : head + 1, rows] = top + jnp.log2(total)
        o_ref[rows, :] = jnp.transpose(jnp.concatenate(outs, axis=0)).astype(o_ref.dtype)
        between(qb)


def attention_forward(q, k, v, factor, size):
    mbs, length, width = q.shape
    lanes = 2 * size
    pairs = width // lanes
    block = pl.BlockSpec((1, length, lanes), lambda m, p: (m, 0, p))
    area = mbs * pairs * 2 * length * (length + QB) // 2
    return pl.pallas_call(
        partial(attention_forward_kernel, factor, size),
        grid=(mbs, pairs),
        in_specs=[block] * 3,
        out_specs=[block, pl.BlockSpec((1, 1, 8, length), lambda m, p: (m, p, 0, 0))],
        out_shape=[
            jax.ShapeDtypeStruct(q.shape, BF16),
            jax.ShapeDtypeStruct((mbs, pairs, 8, length), F32),
        ],
        compiler_params=pltpu.CompilerParams(vmem_limit_bytes=48 << 20),
        cost_estimate=pl.CostEstimate(
            flops=16 * area * size, bytes_accessed=8 * q.size, transcendentals=area
        ),
        name="attention_forward",
    )(q, k, v)


def attention_backward_kernel(factor, size, q_ref, k_ref, v_ref, do_ref, lse_ref, dq_ref, dk_ref, dv_ref, dk_sum, dv_sum):
    refs = [ref.at[0] for ref in (q_ref, k_ref, v_ref, do_ref)]
    attention_backward_block(
        factor, size, *refs, lse_ref.at[0, 0], dq_ref.at[0], dk_ref.at[0], dv_ref.at[0], dk_sum, dv_sum, lambda done: None
    )


def attention_backward_block(
    factor, size, q_ref, k_ref, v_ref, do_ref, lse_ref, dq_ref, dk_ref, dv_ref, dk_sum, dv_sum, between
):
    length = q_ref.shape[0]
    base_two = factor * LOG2E
    k = k_ref[...]
    v = v_ref[...]
    kt = jnp.transpose(k)
    for i, qb in enumerate(reversed(range(length // QB))):
        n = (qb + 1) * QB
        rows = pl.ds(qb * QB, QB)
        q = q_ref[rows, :]
        do = do_ref[rows, :]
        dqs, dk, dv = [], None, None
        for head in range(2):
            qh = head_mask(q, head, size)
            doh = head_mask(do, head, size)
            s = causal(dot_nt(k[:n], qh), qb)
            p = jnp.exp2(s * base_two - lse_ref[head : head + 1, rows])
            dp = dot_nt(v[:n], doh)
            mean = jnp.sum(dp * p, axis=0, keepdims=True)
            ds = (p * (dp - mean)).astype(BF16)
            dvh = dot_nn(p.astype(BF16), doh)
            dkh = dot_nn(ds, qh)
            dv = dvh if dv is None else dv + dvh
            dk = dkh if dk is None else dk + dkh
            dqs.append(dot_nn(kt[head * size : (head + 1) * size, :n], ds))
        dq_ref[rows, :] = jnp.transpose(jnp.concatenate(dqs, axis=0) * factor).astype(BF16)
        if n == length:
            dk_sum[...] = dk
            dv_sum[...] = dv
        else:
            dk_sum[:n] += dk
            dv_sum[:n] += dv
        between(i)
    dk_ref[...] = (dk_sum[...] * factor).astype(BF16)
    dv_ref[...] = dv_sum[...].astype(BF16)


def attention_backward(q, k, v, do, lse, factor, size):
    mbs, length, width = q.shape
    lanes = 2 * size
    pairs = width // lanes
    block = pl.BlockSpec((1, length, lanes), lambda m, p: (m, 0, p))
    area = mbs * pairs * 2 * length * (length + QB) // 2
    return pl.pallas_call(
        partial(attention_backward_kernel, factor, size),
        grid=(mbs, pairs),
        in_specs=[block] * 4 + [pl.BlockSpec((1, 1, 8, length), lambda m, p: (m, p, 0, 0))],
        out_specs=[block] * 3,
        out_shape=[jax.ShapeDtypeStruct(q.shape, BF16)] * 3,
        scratch_shapes=[pltpu.VMEM((length, lanes), F32)] * 2,
        compiler_params=pltpu.CompilerParams(vmem_limit_bytes=48 << 20),
        cost_estimate=pl.CostEstimate(
            flops=40 * area * size, bytes_accessed=14 * q.size, transcendentals=area
        ),
        name="attention_backward",
    )(q, k, v, do, lse)


MESH = pl.DeviceIdType.MESH


def position():
    return lax.axis_index("fsdp"), lax.axis_index("rep"), lax.axis_index("ctx")


def greet(owners, reps):
    z, r, c = position()
    barrier = pltpu.get_barrier_semaphore()
    peers = [{"fsdp": lax.rem(z + j, owners)} for j in range(1, owners)]
    peers += [{"rep": r ^ j} for j in range(1, reps)]
    peers += [{"ctx": 1 - c}]
    for peer in peers:
        pl.semaphore_signal(barrier, inc=1, device_id=peer, device_id_type=MESH)
    pl.semaphore_wait(barrier, len(peers))


def slab(i, half):
    return pl.ds(pl.multiple_of(i * half, 128), half)


def add_blocks(out, parts, dtype):
    lead = out.shape[:-2]
    count = 1
    for n in lead:
        count *= n

    def body(i, _):
        at = []
        for n in reversed(lead):
            at.append(lax.rem(i, n))
            i = lax.div(i, n)
        at = tuple(reversed(at))
        terms = [p[at].astype(F32) for p in parts]
        while len(terms) > 1:
            terms = [terms[0] + terms[1]] + terms[2:]
        out[at] = terms[0].astype(dtype)
        return 0

    lax.fori_loop(0, count, body, 0)


class Plan:
    def __init__(self, send, recv):
        self.send, self.recv = send, recv
        self.made, self.left = {}, set()

    def add(self, name, src, dst, peer):
        self.made[name] = (len(self.made), src, dst, peer)

    def copy(self, name):
        slot, src, dst, peer = self.made[name]
        return pltpu.make_async_remote_copy(
            src_ref=src(),
            dst_ref=dst(),
            send_sem=self.send.at[slot],
            recv_sem=self.recv.at[slot],
            device_id=peer,
            device_id_type=MESH,
        )

    def start(self, *names):
        for name in names:
            self.copy(name).start()

    def arrive(self, *names):
        for name in names:
            self.copy(name).wait_recv()

    def leave(self, *names):
        for name in names:
            self.copy(name).wait_send()
            self.left.add(name)

    def close(self):
        for name in self.made:
            if name not in self.left:
                self.copy(name).wait_send()


def spread_plan(plan, tag, owners, reps, z, r, c, src, dst, halves, core=None):
    for j in range(1, owners):
        origin = lax.rem(z - j + owners, owners)
        if src is not None:
            plan.add((tag, "z", j), src, lambda: dst(z, r), {"fsdp": lax.rem(z + j, owners)})
        here = partial(dst, origin, r)
        plan.add((tag, "x", j), here, here, {"rep": r ^ 1})
        plan.add((tag, "y", j), here, here, {"rep": r ^ 2})
        by_y = lambda origin=origin: halves(dst(origin, r ^ 2))[0]
        by_x = lambda origin=origin: halves(dst(origin, r ^ 1))[1]
        plan.add((tag, "xx", j), by_y, by_y, {"rep": r ^ 1})
        plan.add((tag, "yy", j), by_x, by_x, {"rep": r ^ 2})
        if core is not None:
            side = partial(core, origin)
            plan.add((tag, "c", j), side, side, {"ctx": 1 - c})


def spread_step(plan, tag, owners, stage):
    for j in range(1, owners):
        if stage == 0:
            plan.start((tag, "z", j))
        elif stage == 1:
            if (tag, "z", j) in plan.made:
                plan.arrive((tag, "z", j))
            plan.start((tag, "x", j), (tag, "y", j))
        elif stage == 2:
            plan.arrive((tag, "y", j))
            plan.start((tag, "xx", j))
            plan.arrive((tag, "x", j))
            plan.start((tag, "yy", j))
        elif stage == 3:
            plan.arrive((tag, "xx", j), (tag, "yy", j))
            if (tag, "c", j) in plan.made:
                plan.start((tag, "c", j))
        else:
            plan.arrive((tag, "c", j))


def up_side(ref, c):
    half = ref.shape[-1] // 2
    return ref.at[:, pl.ds(pl.multiple_of(c * half, 128), half)]


def up_piece(ref, c, r):
    return ref.at[:, pl.ds(pl.multiple_of((c * 4 + r) * 128, 128), 128)]


def down_side(ref, c):
    half = ref.shape[0] // 2
    return ref.at[pl.ds(pl.multiple_of(c * half, 32), half)]


def down_piece(ref, c, r):
    piece = ref.shape[0] // 8
    return ref.at[pl.ds(pl.multiple_of((c * 4 + r) * piece, 32), piece)]


def uneven_halves(ref):
    middle = ref.shape[1] // 256 * 128
    return ref.at[:, pl.ds(0, middle)], ref.at[:, pl.ds(middle, ref.shape[1] - middle)]


def row_halves(ref):
    middle = ref.shape[0] // 2
    return ref.at[pl.ds(0, middle)], ref.at[pl.ds(middle, middle)]


def column_halves(ref):
    middle = ref.shape[-1] // 2
    return ref.at[:, pl.ds(0, middle)], ref.at[:, pl.ds(middle, middle)]


SPREADS = [
    (-1, 0, 1), (-1, 1, 1), (2, 2, 1), (5, 0, 2), (9, 1, 2), (9, 0, 3), (14, 2, 2), (14, 1, 3), (15, 0, 4), (18, 1, 4),
    (19, 2, 3), (23, 2, 4),
]


def forward_kernel(owners, reps, pairs, factor, size,
                   x_ref, qkv_ref, mix_ref, up_ref, down_ref, *refs):
    vectors, b_up_ref, refs = refs[:8], refs[8], refs[9:]
    (mixed, qkv_out, first_t_out, w_qkv_out, w_mix, w_up, w_down, vec_ref, bup_ref, lse_ref, small_ref,
                   first, first_t, w_qkv, qkv, heads, small, own_mix, own_up, own_down, send, recv, kept) = refs
    step = pl.program_id(0)
    last = pl.num_programs(0) - 1
    z, r, c = position()
    mbs, rows, width = x_ref.shape
    half = width // 2
    lanes = 2 * size
    plan = Plan(send, recv)
    own_rows = pl.ds(pl.multiple_of(c * rows, rows), rows)
    their_rows = pl.ds(pl.multiple_of((1 - c) * rows, rows), rows)

    for j in range(1, owners):
        plan.add(("small", j), lambda: small_ref, lambda: small.at[z], {"fsdp": lax.rem(z + j, owners)})
    for m in range(mbs):
        plan.add(("first", m), lambda m=m: first.at[m, own_rows], lambda m=m: first.at[m, own_rows], {"ctx": 1 - c})
    for i in range(3):
        spread_plan(
            plan, ("qkv", i), owners, reps, z, r, c,
            lambda i=i: qkv_ref.at[r, :, slab(2 * i + c, half)],
            lambda o, p, i=i: w_qkv.at[o, p, :, slab(i, half)],
            uneven_halves,
        )
    steps = w_up.shape[0]
    spread_plan(
        plan, ("mix", 0), owners, reps, z, r, c,
        lambda: own_mix.at[c, r], lambda o, p: w_mix.at[o, c, p], column_halves, lambda o: w_mix.at[o, c],
    )
    for tag, own, whole, piece, side in (("up", own_up, w_up, up_piece, up_side), ("down", own_down, w_down, down_piece, down_side)):
        for f in range(steps):
            dst = lambda o, p, whole=whole, piece=piece, f=f: piece(whole.at[f, o], c, p)
            src = lambda own=own, piece=piece, f=f: piece(own.at[f], c, r)
            if f == 0:
                core = lambda o, whole=whole, side=side, f=f: side(whole.at[f, o], c)
                spread_plan(plan, (tag, f), owners, reps, z, r, c, src, dst, row_halves, core)
            else:
                for j in range(1, owners):
                    to = lax.rem(z + j, owners)
                    plan.add(((tag, f), "z", j), src, lambda dst=dst: dst(z, r), {"fsdp": to})
    quarters = 2 * rows // QB
    table = SPREADS
    order = [("mix", 0)] + [(tag, f) for f in range(steps) for tag in ("up", "down")]

    up_step = own_up.shape[-1] // owners
    pairs_of = [(small_ref, small.at[z])]
    pairs_of += [(qkv_ref.at[:, :, slab(2 * i + c, half)], w_qkv.at[z, :, :, slab(i, half)]) for i in range(3)]
    pairs_of += [(mix_ref, own_mix)]
    early = len(pairs_of)
    for f in range(steps):
        for k in range(owners):
            cols = pl.ds((k * (up_ref.shape[-1] // owners)) + f * up_step, up_step)
            pairs_of += [(up_ref.at[:, cols], own_up.at[f, :, pl.ds(k * up_step, up_step)])]
        pairs_of += [(down_ref.at[pl.ds(f * own_down.shape[1], own_down.shape[1])], own_down.at[f])]
    loads = len(pairs_of)
    pairs_of += [(own_mix, w_mix.at[z])]
    for f in range(steps):
        pairs_of += [(own_up.at[f], w_up.at[f, z]), (own_down.at[f], w_down.at[f, z])]
    stores = len(pairs_of)
    pairs_of += [(w_qkv, w_qkv_out), (first_t, first_t_out), (qkv, qkv_out)]
    ends = len(pairs_of)

    def keep(i):
        return pltpu.make_async_copy(*pairs_of[i], kept.at[i])

    def mixed_place(step):
        m, p = lax.div(step, pairs), lax.rem(step, pairs)
        return mixed.at[m, :, slab(c * pairs + p, lanes)]

    def mixed_sends(k, slot):
        return pltpu.make_async_remote_copy(
            src_ref=heads.at[k, their_rows],
            dst_ref=mixed_place(k),
            send_sem=send.at[slot],
            recv_sem=recv.at[slot],
            device_id={"ctx": 1 - c},
            device_id_type=MESH,
        )

    base = len(plan.made)

    @pl.when(step == 0)
    def _():
        for i in range(1, loads):
            keep(i).start()
        small_ref[...] = jnp.zeros_like(small_ref)
        own = vectors[0].shape[0]
        for i, vector in enumerate(vectors):
            small_ref[i : i + 1, :own] = vector[...].astype(F32).reshape(1, own)
        for f in range(steps):
            small_ref[8 + f : 9 + f, :] = b_up_ref[f * FP : (f + 1) * FP].astype(F32).reshape(1, FP)
        greet(owners, reps)
        keep(0).start()
        plan.start(*[("small", j) for j in range(1, owners)])
        for i in range(3):
            spread_step(plan, ("qkv", i), owners, 0)
        keep(0).wait()
        plan.arrive(*[("small", j) for j in range(1, owners)])
        vec_ref[...] = jnp.concatenate([small[k, :, :own] for k in range(owners)], axis=1)
        bup_ref[...] = jnp.concatenate([small[k, 8:16] for k in range(owners)], axis=1)
        gain, shift = vec_ref[3:4, :], vec_ref[4:5, :]
        for m in range(mbs):
            for at in range(0, rows, TB):
                normal, _ = norm_stats(x_ref[m, at : at + TB].astype(F32))
                place = pl.ds(pl.multiple_of(c * rows + at, TB), TB)
                first[m, place] = (normal * gain + shift).astype(BF16)
            plan.start(("first", m))
        spread_step(plan, ("qkv", 0), owners, 1)
        for i in range(4, loads):
            keep(i).wait()
        for i in range(loads, stores):
            keep(i).start()
        plan.arrive(*[("first", m) for m in range(mbs)])
        spread_step(plan, ("qkv", 1), owners, 1)
        spread_step(plan, ("qkv", 0), owners, 2)
        spread_step(plan, ("qkv", 2), owners, 1)
        for tag in order[:3]:
            spread_step(plan, tag, owners, 0)

        def turn(i, _):
            m, at = lax.div(i, 2 * rows // TB), lax.rem(i, 2 * rows // TB)
            place = pl.ds(pl.multiple_of(at * TB, TB), TB)
            first_t[:, pl.ds(pl.multiple_of(i * TB, TB), TB)] = jnp.transpose(first[m, place])
            return 0

        lax.fori_loop(0, mbs * 2 * rows // TB, turn, 0)
        keep(stores + 1).start()
        spread_step(plan, ("qkv", 1), owners, 2)

        def project_all(i):
            weight = w_qkv[:, :, :, i * half : (i + 1) * half].reshape(-1, half)
            bias = None if i == 1 else vec_ref[i // 2 : i // 2 + 1, slab(c, half)]

            def project_rows(n, _):
                m, at = lax.div(n, 2 * rows // TB), lax.rem(n, 2 * rows // TB)
                place = pl.ds(pl.multiple_of(at * TB, TB), TB)
                joined = dot_nn(first[m, place], weight)
                joined = (joined if bias is None else joined + bias).astype(BF16)
                for s in range(pairs):
                    qkv[m, i * pairs + s, place] = joined[:, s * lanes : (s + 1) * lanes]
                return 0

            lax.fori_loop(0, mbs * 2 * rows // TB, project_rows, 0)

        for i in range(1, 4):
            keep(i).wait()
        for i in range(3):
            if i == 1:
                spread_step(plan, ("qkv", 2), owners, 2)
            spread_step(plan, ("qkv", i), owners, 3)
            if i == 2:
                for when, t, stage in table:
                    if when < 0:
                        spread_step(plan, order[t], owners, stage)
            project_all(i)
        keep(stores).start()
        keep(stores + 2).start()

    def between(k, done):
        for i in range(mbs * pairs):
            some = [entry for entry in table if entry[0] == i * quarters + done]
            if some:

                @pl.when(k == i)
                def _():
                    for _, t, stage in some:
                        spread_step(plan, order[t], owners, stage)

    @pl.when(step == 1)
    def _():
        for tag in order[3:]:
            spread_step(plan, tag, owners, 0)

    @pl.when(step > 0)
    def _():
        k = step - 1
        m, p = lax.div(k, pairs), lax.rem(k, pairs)
        attention_forward_block(
            factor, size, qkv.at[m, p], qkv.at[m, pairs + p], qkv.at[m, 2 * pairs + p], heads.at[k], lse_ref.at[m, p],
            partial(between, k),
        )
        mixed_sends(k, base + k).start()
        pltpu.make_async_copy(heads.at[k, own_rows], mixed_place(k), kept.at[ends + k]).start()

    @pl.when(step == last)
    def _():
        for when, t, stage in table:
            if when >= quarters * mbs * pairs:
                spread_step(plan, order[t], owners, stage)
        for k in range(mbs * pairs):
            mixed_sends(k, base + k).wait()
            pltpu.make_async_copy(heads.at[k, own_rows], mixed_place(k), kept.at[ends + k]).wait()
        for tag in order[3:]:
            for j in range(1, owners):
                plan.arrive((tag, "z", j))
        plan.close()
        for i in range(loads, ends):
            keep(i).wait()


def forward_block(x, weight_qkv, weight_mix, weight_up, weight_down, vectors, b_up, owners, reps, factor, size):
    own, wide = weight_qkv.shape
    mbs, rows, width = x.shape
    lanes = 2 * size
    pairs = width // 2 // lanes

    def cut(shard):
        return shard.reshape(2, reps, shard.shape[0] // (2 * reps), shard.shape[1])

    steps = weight_down.shape[0] // FP
    shards = (weight_qkv.reshape(reps, own // reps, wide), cut(weight_mix), weight_up, weight_down)
    own_up = (steps, own, owners * FP)
    own_down = (steps, FP, width)
    shape = jax.ShapeDtypeStruct
    w_shape = (owners, reps, own // reps, wide // 2)
    qkv_shape = (mbs, 3 * pairs, 2 * rows, lanes)
    anywhere = pl.BlockSpec(memory_space=pl.ANY)
    whole = lambda s: pl.BlockSpec(s, lambda i: (0,) * len(s), pipeline_mode=pl.Buffered(1))
    remotes = 3 + mbs + 3 * 15 + 3 * 18 + 6 * (steps - 1) + mbs * pairs
    copies = 5 + steps * (owners + 1) + 1 + 2 * steps + 3 + mbs * pairs
    area = mbs * pairs * 2 * rows * (2 * rows + QB)
    mixed, qkv, first_t, w_qkv, w_mix, w_up, w_down, vecs, b_up, lse = pl.pallas_call(
        partial(forward_kernel, owners, reps, pairs, factor, size),
        grid=(1 + mbs * pairs,),
        in_specs=[whole(x.shape)] + [anywhere] * 4 + [whole(v.shape) for v in (*vectors, b_up)],
        out_specs=[anywhere] * 7 + [whole((16, width)), whole((8, owners * FP)), whole((mbs, pairs, 8, 2 * rows))],
        out_shape=[
            shape((mbs, rows, width), BF16),
            shape(qkv_shape, BF16),
            shape((width, mbs * 2 * rows), BF16),
            shape(w_shape, BF16),
            shape((owners,) + shards[1].shape, BF16),
            shape(own_up[:1] + (owners,) + own_up[1:], BF16),
            shape(own_down[:1] + (owners,) + own_down[1:], BF16),
            shape((16, width), F32),
            shape((8, owners * FP), F32),
            shape((mbs, pairs, 8, 2 * rows), F32),
        ],
        scratch_shapes=[
            pltpu.VMEM((16, FP), F32),
            pltpu.VMEM((mbs, 2 * rows, width), BF16),
            pltpu.VMEM((width, mbs * 2 * rows), BF16),
            pltpu.VMEM(w_shape, BF16),
            pltpu.VMEM(qkv_shape, BF16),
            pltpu.VMEM((mbs * pairs, 2 * rows, lanes), BF16),
            pltpu.VMEM((owners, 16, FP), F32),
            pltpu.VMEM(shards[1].shape, BF16),
            pltpu.VMEM(own_up, BF16),
            pltpu.VMEM(own_down, BF16),
            pltpu.SemaphoreType.DMA((remotes,)),
            pltpu.SemaphoreType.DMA((remotes,)),
            pltpu.SemaphoreType.DMA((copies,)),
        ],
        compiler_params=pltpu.CompilerParams(
            collective_id=1, has_side_effects=True, vmem_limit_bytes=56 << 20
        ),
        name="forward_block",
    )(x, *shards, *vectors, b_up)
    return (
        mixed,
        qkv,
        first_t,
        w_qkv.reshape(owners * own, -1),
        w_mix.reshape(owners * own, -1),
        w_up,
        w_down,
        vecs,
        b_up[:steps].reshape(steps, 1, owners * FP),
        lse,
    )


class Flow:
    def __init__(self, plan, name, place, owners, bits, mine, theirs, hops, outs, load=None, core=None):
        z, r, c = place
        first, second = bits
        self.plan, self.name, self.place, self.owners = plan, name, place, owners
        self.mine, self.theirs, self.second = mine, theirs, r ^ second
        self.hop_one, self.hop_two, self.hop_z, self.final = hops
        self.outs = outs
        self.load = load
        peer = {"rep": r ^ first}
        if core is not None:
            plan.add((name, "core"), core, lambda: theirs, {"ctx": 1 - c})
        self.split = core is not None
        plan.add((name, "me"), lambda: mine.at[:, r ^ first], lambda: self.hop_one.at[0], peer)
        plan.add((name, "on"), lambda: mine.at[:, r ^ first ^ second], lambda: self.hop_one.at[1], peer)
        plan.add((name, "two"), lambda: mine.at[:, r ^ second], lambda: self.hop_two, {"rep": r ^ second})
        for j in range(1, owners):
            to = lax.rem(z + j, owners)
            plan.add((name, "z", j), lambda to=to: mine.at[to, r], lambda j=j: self.hop_z.at[j - 1], {"fsdp": to})
        here = lambda: self.final.at[c, r]
        plan.add((name, "x"), here, here, {"rep": r ^ first})
        plan.add((name, "y"), here, here, {"rep": r ^ second})
        far = lambda: self.final.at[c, r ^ second]
        plan.add((name, "xy"), far, far, {"rep": r ^ first})
        side = lambda: self.final.at[c]
        plan.add((name, "back"), side, side, {"ctx": 1 - c})

    def step(self, stage):
        z, r, c = self.place
        plan, name, mine = self.plan, self.name, self.mine
        owners = self.owners
        if stage == 0:
            if self.split:
                plan.start((name, "core"))
            if self.load is not None:
                self.load().start()
        elif stage == 1:
            if self.load is not None:
                self.load().wait()
            if self.split:
                plan.arrive((name, "core"))
                add_blocks(mine, [mine, self.theirs], BF16)
            plan.start((name, "on"), (name, "me"))
        elif stage == 2:
            plan.arrive((name, "on"))
            part = mine.at[:, self.second]
            add_blocks(part, [part, self.hop_one.at[1]], BF16)
            plan.start((name, "two"))
        elif stage == 3:
            plan.arrive((name, "me"), (name, "two"))
            part = mine.at[:, r]
            add_blocks(part, [part, self.hop_one.at[0], self.hop_two], BF16)
            plan.start(*[(name, "z", j) for j in range(1, owners)])
        elif stage == 4:
            plan.arrive(*[(name, "z", j) for j in range(1, owners)])
            terms = [mine[z, r].astype(F32)] + [self.hop_z[j].astype(F32) for j in range(owners - 1)]
            while len(terms) > 1:
                terms = [a + b for a, b in zip(terms[::2], terms[1::2])]
            self.final[c, r] = terms[0].astype(BF16)
            plan.start((name, "x"), (name, "y"))
        elif stage == 5:
            plan.arrive((name, "y"))
            plan.start((name, "xy"))
        elif stage == 6:
            plan.arrive((name, "x"), (name, "xy"))
            plan.start((name, "back"))
        else:
            plan.arrive((name, "back"))
            for copy in self.outs(self.final):
                copy.start()


def flow_scratch(owners, reps, piece, split):
    vmem = lambda *lead: pltpu.VMEM(lead + piece, BF16)
    mine = [vmem(owners, reps)] * (2 if split else 1)
    return mine + [vmem(2, owners), vmem(owners), vmem(owners - 1), vmem(2, reps)]


def timetable(groups, products):
    table = []
    for g in range(groups):
        second = 6 + 4 * g
        times = (1 + 2 * g, second, second + 5, second + 9, second + 11, second + 13, second + 15)
        table += [(t, g, 1 + i) for i, t in enumerate(times)]
    for p, second in zip(range(products), (20, 27, 28)):
        times = (second, second + 4, second + 8, second + 10, second + 12, second + 14)
        table += [(t, groups + p, 2 + i) for i, t in enumerate(times)]
    return sorted(table)


def gelu_parts(b):
    square = b * b
    inner = GELU_A * b * (1.0 + GELU_B * square)
    t = jnp.tanh(inner)
    rise = 0.5 * (1.0 + t)
    slope = rise + 0.5 * b * (1.0 - t * t) * (GELU_A * (1.0 + 3.0 * GELU_B * square))
    return b * rise, slope


GATHERS = [
    (1, ("up", 1), 2), (1, ("down", 1), 2), (2, ("up", 1), 3), (2, ("down", 1), 3), (2, ("up", 2), 1), (2, ("down", 2), 1),
    (4, ("up", 1), 4), (4, ("down", 1), 4), (5, ("up", 2), 2), (5, ("down", 2), 2), (6, ("up", 2), 3), (6, ("down", 2), 3),
    (8, ("up", 2), 4), (8, ("down", 2), 4),
]
SUMS = [
    (3, 0, 0), (3, 1, 0), (5, 0, 1), (6, 1, 1), (8, 0, 2), (9, 1, 2), (9, 0, 3), (10, 1, 3), (10, 0, 4), (11, 0, 5),
    (11, 1, 4), (12, 1, 5), (12, 0, 6), (13, 1, 6), (14, 0, 7), (14, 1, 7),
]


def middle_kernel(owners, reps, direct, *refs):
    x_ref, mixed_ref, d_ref, wmix_ref, wup_any, wdown_any, vec_ref, bup_ref = refs[:8]
    result_ref, dmid_ref, dmixed_ref, gmix_ref, gup_ref, gdown_ref, gvec_ref = refs[8:15]
    refs = refs[15:]
    if direct:
        down_out, up_out, refs = refs[0], refs[1], refs[2:]
    middle, second, second_t, mixed_t, out_sum, ds_sum, active_t, d_before, w_up, w_down = refs[:10]
    refs = refs[10:]
    step = pl.program_id(0)
    rows = x_ref.shape[0]
    steps = w_up.shape[0]
    last = steps - 1
    count = rows // TB
    chunk = lambda i: pl.ds(pl.multiple_of(i * TB, TB), TB)
    b_mix, gain, shift, b_down = (vec_ref[i : i + 1, :] for i in (2, 5, 6, 7))
    slots = 4

    if direct:
        flow_refs, (send, recv, kept) = refs[:-3], refs[-3:]
        place = z, r, c = position()
        plan = Plan(send, recv)
        used = 0

        def local(src, dst):
            nonlocal used
            used += 1
            slot = kept.at[used - 1]
            return lambda: pltpu.make_async_copy(src(), dst(), slot)

        own_rows, part = w_up.shape[1] // owners, w_down.shape[1] // owners
        up_of = lambda ref, f, o: ref.at[f, pl.ds(pl.multiple_of(o * own_rows, 32), own_rows)]
        down_of = lambda ref, f, o: ref.at[f, pl.ds(pl.multiple_of(o * part, 32), part)]
        loads, pieces = [], {}
        for tag, source, whole, of, piece, side in (
            ("up", wup_any, w_up, up_of, up_piece, up_side),
            ("down", wdown_any, w_down, down_of, down_piece, down_side),
        ):
            for o in range(owners):
                loads.append(local(lambda o=o, s=source: s.at[0, o], lambda o=o, w=whole, of=of: of(w, 0, o)))
            for f in range(1, steps):
                loads.append(
                    local(lambda f=f, s=source: s.at[f, z], lambda f=f, w=whole, of=of: of(w, f, z))
                )
                pieces[tag, f] = [
                    local(
                        lambda f=f, j=j, s=source, p=piece: p(s.at[f, lax.rem(z + j, owners)], c, r),
                        lambda f=f, j=j, w=whole, of=of, p=piece: p(of(w, f, lax.rem(z + j, owners)), c, r),
                    )
                    for j in range(1, owners)
                ]
                spread_plan(
                    plan, (tag, f), owners, reps, z, r, c, None,
                    lambda o, p, f=f, w=whole, of=of, piece=piece: piece(of(w, f, o), c, p),
                    row_halves,
                    lambda o, f=f, w=whole, of=of, side=side: side(of(w, f, o), c),
                )
        flows, leaving, at = [], [], 0
        for i, (ref, out) in enumerate(((gdown_ref, down_out), (gup_ref, up_out))):
            wide = ref.shape[-1] // 2
            up_step = ref.shape[-1] // owners
            for s in range(2):
                mine, theirs, *hops = flow_refs[at : at + 6]
                at += 6
                cols, final = pl.ds(s * wide, wide), hops[-1]
                if i == 1:
                    places = []
                    for k in range(wide // up_step):
                        to = pl.ds((s * wide // up_step + k) * steps * up_step, up_step)
                        places.append((
                            lambda final=final, k=k: final.at[:, :, :, pl.ds(k * up_step, up_step)],
                            lambda out=out, to=to: out.at[:, :, :, to],
                        ))
                else:
                    places = [(lambda final=final: final, lambda out=out, cols=cols: out.at[0, :, :, :, cols])]
                copies = [local(src, dst) for src, dst in places]
                leaving.extend(copies)
                flows.append(
                    Flow(
                        plan, (i, s), place, owners, (1, 2) if s == 0 else (2, 1), mine, theirs, hops,
                        lambda final, copies=copies: [f() for f in copies],
                        local(lambda ref=ref, cols=cols: ref.at[0, :, c, :, :, cols], lambda mine=mine: mine),
                        lambda ref=ref, cols=cols: ref.at[0, :, 1 - c, :, :, cols],
                    )
                )
    else:
        kept = refs[0]
        loads = [
            lambda: pltpu.make_async_copy(wup_any, w_up, kept.at[0]),
            lambda: pltpu.make_async_copy(wdown_any, w_down, kept.at[1]),
        ]

    def between(slot, here=True):
        if not direct:
            return
        for k in range(steps):
            some = [lambda t=t, n=n: spread_step(plan, t, owners, n) for when, t, n in GATHERS if when == k * slots + slot]
            some += [lambda g=g, n=n: [flow.step(n) for flow in flows[2 * g : 2 * g + 2]] for when, g, n in SUMS if when == k * slots + slot]
            if some:

                @pl.when((step == k) & here)
                def _():
                    for act in some:
                        act()

    @pl.when(step == 0)
    def _():
        for copy in loads:
            copy().start()
        if direct:
            for some in pieces.values():
                for copy in some:
                    copy().start()
            greet(owners, reps)
            for f in range(1, steps):
                for tag in ("up", "down"):
                    for copy in pieces[tag, f]:
                        copy().wait()
                    if f == 1:
                        spread_step(plan, (tag, f), owners, 1)
        gvec_ref[...] = jnp.zeros_like(gvec_ref)

        def prepare(i, _):
            at = chunk(i)
            mixed = mixed_ref[at]
            mixed_t[:, at] = jnp.transpose(mixed)
            mid = x_ref[at].astype(F32) + (dot_nn(mixed, wmix_ref[...]) + b_mix)
            middle[at] = mid
            out_sum[at] = mid + b_down
            ds_sum[at] = jnp.zeros_like(mid)
            normal, _ = norm_stats(mid)
            low = (normal * gain + shift).astype(BF16)
            second[at] = low
            second_t[:, at] = jnp.transpose(low)
            return 0

        lax.fori_loop(0, count, prepare, 0)
        for copy in loads:
            copy().wait()

    between(0)

    def feed(i, d_bup):
        at = chunk(i)
        act, slope = gelu_parts(dot_nn(second[at], w_up[step]) + bup_ref[0])
        act = act.astype(BF16)
        active_t[:, at] = jnp.transpose(act)
        db = (dot_nt(d_ref[at], w_down[step]) * slope).astype(BF16)
        d_before[at] = db
        out_sum[at] += dot_nn(act, w_down[step])
        ds_sum[at] += dot_nt(db, w_up[step])
        between(1, i == count // 2 - 1)
        return d_bup + jnp.sum(db.astype(F32), axis=0, keepdims=True)

    d_bup = lax.fori_loop(0, count, feed, jnp.zeros(bup_ref.shape[1:], F32))
    between(2)

    width = d_bup.shape[1] // owners
    for k in range(owners):
        gvec_ref[8 + k : 9 + k, slab(step, width)] = d_bup[:, k * width : (k + 1) * width]
    if direct:

        @pl.when(step == 1)
        def _():
            plan.leave(*[(flow.name, "core") for flow in flows])

    share = second_t.shape[0] // owners
    part = active_t.shape[0] // owners

    def weights(o, _):
        lines = pl.ds(pl.multiple_of(o * part, part), part)
        gdown_ref[0, o] = dot_nn(active_t[lines], d_ref[...]).reshape(gdown_ref.shape[2:]).astype(BF16)
        lines = pl.ds(pl.multiple_of(o * share, 64), share)
        gup_ref[0, o] = dot_nn(second_t[lines], d_before[...]).reshape(gup_ref.shape[2:]).astype(BF16)
        return 0

    lax.fori_loop(0, owners, weights, 0)
    between(slots - 1)

    @pl.when(step == last)
    def _():

        def finish(i, sums):
            at = chunk(i)
            result_ref[at] = out_sum[at].astype(BF16)
            normal, inverse = norm_stats(middle[at])
            ds = ds_sum[at]
            grad_out = d_ref[at].astype(F32)
            d_mid = grad_out + norm_back(ds, normal, inverse, gain)
            dmid_ref[at] = d_mid
            branch = d_mid.astype(BF16)
            second[at] = branch
            dmixed_ref[at] = dot_nt(branch, wmix_ref[...]).astype(BF16)
            parts = (branch.astype(F32), ds * normal, ds, grad_out)
            return tuple(s + jnp.sum(p, axis=0, keepdims=True) for s, p in zip(sums, parts))

        zero = jnp.zeros((1, x_ref.shape[1]), F32)
        sums = lax.fori_loop(0, count, finish, (zero,) * 4)
        for i, k in enumerate((2, 5, 6, 7)):
            gvec_ref[k : k + 1, :] = sums[i]

        def mix(o, _):
            lines = pl.ds(pl.multiple_of(o * share, 64), share)
            gmix_ref[o] = dot_nn(mixed_t[lines], second[...]).reshape(gmix_ref.shape[1:]).astype(BF16)
            return 0

        lax.fori_loop(0, owners, mix, 0)
        if direct:
            for when, g, n in SUMS:
                if when >= steps * slots:
                    for flow in flows[2 * g : 2 * g + 2]:
                        flow.step(n)
            plan.close()
            for copy in leaving:
                copy().wait()


def middle_block(x, mixed, d_out, w_mix, w_up, w_down, vecs, b_up, owners, reps, direct):
    rows, width = x.shape
    steps = w_up.shape[0]
    ff = steps * owners * FP
    whole = lambda shape: pl.BlockSpec(shape, lambda f: (0,) * len(shape), pipeline_mode=pl.Buffered(1))
    anywhere = pl.BlockSpec(memory_space=pl.ANY)
    out = jax.ShapeDtypeStruct
    vmem = pltpu.VMEM
    side = (owners, 2, reps)
    g_mix = side + (width // owners // 2 // reps, width)
    given = steps - 1 if direct else steps
    g_up = (given,) + g_mix[:-1] + (owners * FP,)
    g_down = (given,) + side + (FP // 2 // reps, width)
    skip = steps - given
    per_step = lambda s: pl.BlockSpec((1,) + s[1:], lambda f: (jnp.maximum(f - skip, 0),) + (0,) * (len(s) - 1))
    scratch = [
        vmem((rows, width), F32),
        vmem((rows, width), BF16),
        vmem((width, rows), BF16),
        vmem((width, rows), BF16),
        vmem((rows, width), F32),
        vmem((rows, width), F32),
        vmem((owners * FP, rows), BF16),
        vmem((rows, owners * FP), BF16),
        vmem((steps, width, owners * FP), BF16),
        vmem((steps, owners * FP, width), BF16),
    ]
    finished = []
    if direct:
        finished = [out((steps,) + g_down[2:], BF16), out(g_up[2:5] + (steps * g_up[5],), BF16)]
        for g in (g_down, g_up):
            for _ in range(2):
                scratch += flow_scratch(owners, reps, (g[4], g[5] // 2), True)
        remotes = (steps - 1) * 2 * 15 + 4 * 11
        scratch += [pltpu.SemaphoreType.DMA((remotes,))] * 2 + [pltpu.SemaphoreType.DMA((2 * owners + 2 * (steps - 1) * owners + 10,))]
        params = dict(collective_id=3, has_side_effects=True)
    else:
        scratch += [pltpu.SemaphoreType.DMA((2,))]
        params = {}
    return pl.pallas_call(
        partial(middle_kernel, owners, reps, direct),
        grid=(steps,),
        in_specs=[whole((rows, width))] * 3
        + [whole((width, width)), anywhere, anywhere, whole(vecs.shape), pl.BlockSpec((1, 1, owners * FP), lambda f: (f, 0, 0))],
        out_specs=[
            whole((rows, width)),
            whole((rows, width)),
            whole((rows, width)),
            whole(g_mix),
            per_step(g_up),
            per_step(g_down),
            whole((16, width)),
        ]
        + [anywhere] * len(finished),
        out_shape=[
            out((rows, width), BF16),
            out((rows, width), F32),
            out((rows, width), BF16),
            out(g_mix, BF16),
            out(g_up, BF16),
            out(g_down, BF16),
            out((16, width), F32),
        ]
        + finished,
        scratch_shapes=scratch,
        compiler_params=pltpu.CompilerParams(vmem_limit_bytes=62 << 20, **params),
        cost_estimate=pl.CostEstimate(
            flops=12 * rows * width * ff + 6 * rows * width * width,
            bytes_accessed=8 * width * ff + 16 * rows * width,
            transcendentals=rows * ff,
        ),
        name="middle_block",
    )(x, mixed, d_out, w_mix, w_up, w_down, vecs, b_up)


def backward_kernel(
    owners, reps, pairs, factor, size, shapes, done,
    q_ref, k_ref, v_ref, lse_ref, x_ref, vec_ref, gvec_ref, dmid_ref, dmixed_ref, first_t_ref, w_ref, *refs
):
    n_in = len(shapes)
    sources, refs = refs[:n_in], refs[n_in + 2 :]
    dtok_ref, vec_out, refs = refs[0], refs[1], refs[2:]
    outs, refs = refs[: n_in + 1], refs[n_in + 1 :]
    d_heads, d_joined, first_t, w_pairs, df_send, df_recv, dk_sum, dv_sum, b_sum, vec_one, vec_got, vec_sum, refs = (
        refs[:12] + (refs[12:],)
    )
    flow_refs, (send, recv, kept) = refs[:-3], refs[-3:]
    step = pl.program_id(0)
    last = pl.num_programs(0) - 1
    place = z, r, c = position()
    mbs, rows, width = x_ref.shape
    half = width // 2
    lanes = 2 * size
    plan = Plan(send, recv)
    own_rows = pl.ds(pl.multiple_of(c * rows, rows), rows)

    locals_used = 0

    def local(src, dst):
        nonlocal locals_used
        locals_used += 1
        slot = kept.at[locals_used - 1]
        return lambda: pltpu.make_async_copy(src(), dst(), slot)

    up_step = shapes[1][-1] // owners
    flows, leaving, at = [], [], 0

    def add_flow(name, bits, mine, theirs, hops, places, load=None, core=None):
        final = hops[-1]
        copies = [local(partial(part, final), dst) for part, dst in places]
        leaving.extend(copies)
        flows.append(
            Flow(plan, name, place, owners, bits, mine, theirs, hops, lambda final: [f() for f in copies], load, core)
        )

    for i, shape in enumerate(shapes):
        for f in range(shape[0]):
            wide = shape[-1] // 2
            for s in range(2):
                mine, theirs, *hops = flow_refs[at : at + 6]
                at += 6
                source, out, cols = sources[i], outs[i], pl.ds(s * wide, wide)
                if i == 1:
                    places = []
                    for k in range(wide // up_step):
                        to = pl.ds(((s * wide // up_step + k) * (shape[0] + done) + done + f) * up_step, up_step)
                        places.append((
                            lambda final, k=k: final.at[:, :, :, pl.ds(k * up_step, up_step)],
                            lambda out=out, to=to: out.at[:, :, :, to],
                        ))
                else:
                    skip = done if i == 0 else 0
                    places = [(lambda final: final, lambda out=out, f=f + skip, cols=cols: out.at[f, :, :, :, cols])]
                add_flow(
                    (i, f, s), (1, 2) if s == 0 else (2, 1), mine, theirs, hops, places,
                    local(lambda source=source, f=f, cols=cols: source.at[f, :, c, :, :, cols], lambda mine=mine: mine),
                    lambda source=source, f=f, cols=cols: source.at[f, :, 1 - c, :, :, cols],
                )
    for p in range(pairs):
        for s in range(2):
            mine, *hops = flow_refs[at : at + 5]
            at += 5
            places = []
            for side in range(2):
                for i in range(3):
                    to = pl.ds((i * 2 * pairs + side * pairs + p) * lanes, lanes)
                    places.append((
                        lambda final, side=side, i=i: final.at[side, :, :, pl.ds(i * lanes, lanes)],
                        lambda s=s, to=to: outs[-1].at[:, s, :, to],
                    ))
            add_flow((n_in, p, s), (1, 2) if s == 0 else (2, 1), mine, None, hops, places)
    groups = [flows[i : i + 2] for i in range(0, len(flows), 2)]
    products = len(groups) - pairs
    ff_steps = shapes[0][0]
    groups[: 2 * ff_steps] = [groups[k * ff_steps + f] for f in range(ff_steps) for k in range(2)]

    def advance(group, stage):
        for flow in groups[group]:
            flow.step(stage)

    for m in range(mbs):
        for p in range(pairs):
            plan.add(
                ("heads", m, p),
                lambda m=m, p=p: dmixed_ref.at[m, :, slab((1 - c) * pairs + p, lanes)],
                lambda m=m, p=p: d_heads.at[p, m, own_rows],
                {"ctx": 1 - c},
            )
        plan.add(("first", m), lambda m=m: df_send.at[m], lambda m=m: df_recv.at[m], {"ctx": 1 - c})
    for i, peer in enumerate([{"ctx": 1 - c}, {"rep": r ^ 1}, {"rep": r ^ 2}]):
        plan.add(("vec", i), lambda i=i: vec_sum.at[i], lambda i=i: vec_got.at[i], peer)
    for j in range(1, owners):
        plan.add(
            ("vec", "z", j), lambda: vec_sum.at[3], lambda j=j: vec_got.at[2 + j], {"fsdp": lax.rem(z + j, owners)}
        )

    def own_heads(m, p):
        return pltpu.make_async_copy(
            dmixed_ref.at[m, :, slab(c * pairs + p, lanes)], d_heads.at[p, m, own_rows], kept.at[locals_used + m * pairs + p]
        )

    def load_first():
        return pltpu.make_async_copy(first_t_ref, first_t, kept.at[locals_used + mbs * pairs])

    def load_weight(i, p):
        return pltpu.make_async_copy(
            w_ref.at[:, pl.ds((i * pairs + p) * lanes, lanes)],
            w_pairs.at[p, :, pl.ds(i * lanes, lanes)],
            kept.at[locals_used + mbs * pairs + 1 + i * pairs + p],
        )

    @pl.when(step == 0)
    def _():
        greet(owners, reps)
        for p in range(pairs):
            for m in range(mbs):
                plan.start(("heads", m, p))
                own_heads(m, p).start()
        for g in range(products):
            advance(g, 0)
        load_first().start()
        for i in range(3):
            for p in range(pairs):
                load_weight(i, p).start()
        for p in range(pairs):
            for m in range(mbs):
                plan.arrive(("heads", m, p))
                own_heads(m, p).wait()

    table = timetable(products, pairs)
    quarters = 2 * rows // QB
    tail = [entry for entry in table if entry[0] >= quarters * mbs * pairs]

    def between(k, done):
        for i in range(mbs * pairs):
            some = [entry for entry in table if entry[0] == quarters * i + done]
            if some:

                @pl.when(k == i)
                def _():
                    for _, group, stage in some:
                        advance(group, stage)

    def weight_grad(p):
        grad = dot_nn(first_t[...], d_joined[p])
        piece = groups[products][0].mine.shape[2]
        grad = grad.reshape(owners, reps, 2 * piece, grad.shape[1])
        for s in range(2):
            groups[products + p][s].mine[...] = grad[:, :, s * piece : (s + 1) * piece].astype(BF16)

    for p in range(pairs):

        @pl.when(step == mbs * (p + 1))
        def _():
            if p == 0:
                load_first().wait()
            weight_grad(p)
            advance(products + p, 1)

    @pl.when(step < last)
    def _():
        p, m = lax.div(step, mbs), lax.rem(step, mbs)
        start = pl.multiple_of(m * 2 * rows, 2 * rows)
        joined = d_joined.at[p, pl.ds(start, 2 * rows)]
        attention_backward_block(
            factor, size, q_ref.at[0, 0], k_ref.at[0, 0], v_ref.at[0, 0], d_heads.at[p, m], lse_ref.at[m, p],
            joined.at[:, pl.ds(0, lanes)], joined.at[:, pl.ds(lanes, lanes)], joined.at[:, pl.ds(2 * lanes, lanes)],
            dk_sum, dv_sum, partial(between, step),
        )
        for i, k in enumerate((0, 2)):
            part = jnp.sum(joined[:, k * lanes : (k + 1) * lanes].astype(F32), axis=0, keepdims=True)
            before = b_sum[p, i : i + 1, :]
            b_sum[p, i : i + 1, :] = part + jnp.where(m == 0, jnp.zeros_like(before), before)

    def first_part(m, at):
        total = None
        for p in range(pairs):
            term = dot_nt(d_joined[p, pl.ds(pl.multiple_of(m * 2 * rows + at, TB), TB)], w_pairs[p])
            total = term if total is None else total + term
        return total

    @pl.when(step == last)
    def _():
        for i in range(3):
            for p in range(pairs):
                load_weight(i, p).wait()
        gain = vec_ref[3:4, :]
        steps = rows // TB

        def theirs(i, _):
            m, at = lax.div(i, steps), lax.rem(i, steps) * TB
            df_send[m, pl.ds(pl.multiple_of(at, TB), TB)] = first_part(m, (1 - c) * rows + at).astype(BF16)
            return 0

        def go(until):
            while tail and tail[0][0] < until:
                _, group, stage = tail.pop(0)
                advance(group, stage)

        lax.fori_loop(0, mbs * steps, theirs, 0)
        for m in range(mbs):
            plan.start(("first", m))
        go(28)
        for m in range(mbs):
            plan.arrive(("first", m))

        def mine(i, sums):
            m, at = lax.div(i, steps), lax.rem(i, steps) * TB
            here = pl.ds(pl.multiple_of(at, TB), TB)
            total = first_part(m, c * rows + at) + df_recv[m, here].astype(F32)
            normal, inverse = norm_stats(x_ref[m, here].astype(F32))
            dtok_ref[m, here] = dmid_ref[m, here] + norm_back(total, normal, inverse, gain)
            gains = jnp.sum(total * normal, axis=0, keepdims=True)
            return (sums[0] + gains, sums[1] + jnp.sum(total, axis=0, keepdims=True))

        zero = jnp.zeros((1, width), F32)
        g_gain, g_shift = lax.fori_loop(0, mbs * steps, mine, (zero, zero))
        vec_one[...] = gvec_ref[...]
        vec_one[3:4, :] = g_gain
        vec_one[4:5, :] = g_shift
        for p in range(pairs):
            for i in range(2):
                vec_one[i : i + 1, slab(c * pairs + p, lanes)] = b_sum[p, i : i + 1, :]
        vec_sum[0] = vec_one[...]
        plan.start(("vec", 0))
        for i in range(3):
            go(36 + 2 * i)
            plan.arrive(("vec", i))
            vec_sum[i + 1] = vec_sum[i] + vec_got[i]
            if i < 2:
                plan.start(("vec", i + 1))
        plan.start(*[("vec", "z", j) for j in range(1, owners)])
        go(42)
        plan.arrive(*[("vec", "z", j) for j in range(1, owners)])
        vec_out[...] = (vec_sum[3] + vec_got[3]) + (vec_got[4] + vec_got[5])
        go(1000)
        plan.close()
        for copy in leaving:
            copy().wait()


def backward_block(
    qkv, lse, x, vecs, gvec, d_middle, d_mixed, first_t, w_qkv, grads, finished, owners, reps, factor, size
):
    mbs, rows, width = x.shape
    lanes = 2 * size
    pairs = width // 2 // lanes
    shape = jax.ShapeDtypeStruct
    anywhere = pl.BlockSpec(memory_space=pl.ANY)
    whole = lambda s: pl.BlockSpec(s, lambda i: (0,) * len(s), pipeline_mode=pl.Buffered(1))
    final_step = mbs * pairs - 1

    def block(which):
        def index(i):
            k = jnp.minimum(i, final_step)
            return (lax.rem(k, mbs), which * pairs + lax.div(k, mbs), 0, 0)

        return pl.BlockSpec((1, 1, 2 * rows, lanes), index)

    pieces = [(g.shape[4], g.shape[5] // 2) for g in grads for _ in range(2 * g.shape[0])]
    q_piece = (width // owners // reps // 2, 3 * lanes)
    down, up, mix = (g.shape for g in grads)
    finals = [f.shape for f in finished] + [mix[:1] + mix[2:], (reps, 2, q_piece[0], 3 * width)]
    scratch = [s for p in pieces for s in flow_scratch(owners, reps, p, True)]
    scratch += [s for _ in range(2 * pairs) for s in flow_scratch(owners, reps, q_piece, False)]
    remotes = 11 * len(pieces) + 10 * 2 * pairs + mbs * pairs + mbs + 6
    vec = (16, width)
    dtok, vec_sum, *outs = pl.pallas_call(
        partial(backward_kernel, owners, reps, pairs, factor, size, [g.shape for g in grads], finished[0].shape[0] - down[0]),
        grid=(mbs * pairs + 1,),
        in_specs=[block(0), block(1), block(2), whole(lse.shape), whole(x.shape), whole(vec), whole(vec), whole(x.shape)]
        + [anywhere] * (3 + len(grads) + 2),
        input_output_aliases={11 + len(grads): 2, 12 + len(grads): 3},
        out_specs=[whole(x.shape), whole(vec)] + [anywhere] * len(finals),
        out_shape=[shape(x.shape, F32), shape(vec, F32)] + [shape(f, BF16) for f in finals],
        scratch_shapes=[
            pltpu.VMEM((pairs, mbs, 2 * rows, lanes), BF16),
            pltpu.VMEM((pairs, mbs * 2 * rows, 3 * lanes), BF16),
            pltpu.VMEM(first_t.shape, BF16),
            pltpu.VMEM((pairs, width, 3 * lanes), BF16),
            pltpu.VMEM(x.shape, BF16),
            pltpu.VMEM(x.shape, BF16),
            pltpu.VMEM((2 * rows, lanes), F32),
            pltpu.VMEM((2 * rows, lanes), F32),
            pltpu.VMEM((pairs, 8, lanes), F32),
            pltpu.VMEM(vec, F32),
            pltpu.VMEM((6,) + vec, F32),
            pltpu.VMEM((4,) + vec, F32),
        ]
        + scratch
        + [
            pltpu.SemaphoreType.DMA((remotes,)),
            pltpu.SemaphoreType.DMA((remotes,)),
            pltpu.SemaphoreType.DMA((len(pieces) * 3 + 12 * pairs + mbs * pairs + 1 + 3 * pairs,)),
        ],
        compiler_params=pltpu.CompilerParams(
            collective_id=2, has_side_effects=True, vmem_limit_bytes=63 << 20
        ),
        name="backward_block",
    )(qkv, qkv, qkv, lse, x, vecs, gvec, d_middle, d_mixed, first_t, w_qkv, *grads, *finished)
    return dtok, vec_sum, outs


def local(
    inputs,
    weight_qkv,
    bias_query,
    bias_value,
    weight_mix,
    bias_mix,
    gain_attn,
    shift_attn,
    gain_mlp,
    shift_mlp,
    weight_up,
    bias_up,
    weight_down,
    bias_down,
    cotangent,
):
    width = weight_qkv.shape[1] // 3
    half = width // 2
    size = width // H
    factor = size ** (-0.5)
    rows = inputs.shape[2]
    owners = lax.axis_size("fsdp")
    reps = lax.axis_size("rep")
    ctx = lax.axis_index("ctx")
    rep = lax.axis_index("rep")
    own = weight_qkv.shape[0]
    b_up_rows = bias_up.shape[0]
    direct = own % (16 * reps) == 0 and owners == 4 and reps == 4

    def swap(x):
        return lax.ppermute(x, "ctx", [(0, 1), (1, 0)])

    def order(mine, other, axis):
        return jnp.where(
            ctx == 0,
            jnp.concatenate([mine, other], axis=axis),
            jnp.concatenate([other, mine], axis=axis),
        )

    def columns(x, axis, which):
        return lax.dynamic_slice_in_dim(x, which * half, half, axis)

    direct = own % (16 * reps) == 0 and owners == 4 and reps == 4
    vectors = [bias_query, bias_value, bias_mix, gain_attn, shift_attn, gain_mlp, shift_mlp, bias_down]
    tokens = inputs[:, 0].astype(F32)
    if direct:
        mixed, qkv, first_t, w_qkv, w_mix, w_up, w_down, vecs, b_up, lse = forward_block(
            inputs[:, 0],
            weight_qkv,
            weight_mix,
            weight_up,
            weight_down,
            vectors,
            bias_up,
            owners,
            reps,
            factor,
            size,
        )
    else:
        part = own // reps
        mine = lax.dynamic_slice_in_dim(weight_qkv, rep * part, part, 0)
        mine = jnp.concatenate([columns(mine[:, i * width : (i + 1) * width], 1, ctx) for i in range(3)], axis=1)
        w_qkv = lax.all_gather(mine, ("fsdp", "rep"), axis=0, tiled=True)

        def gather(shard):
            piece = shard.shape[0] // (2 * reps)
            mine = lax.dynamic_slice_in_dim(shard, (rep * 2 + ctx) * piece, piece, 0)
            return lax.all_gather(mine, ("fsdp", "rep", "ctx"), axis=0, tiled=True)

        w_mix = gather(weight_mix)
        w_up = gather(weight_up)
        w_down = gather(weight_down)
        vecs = lax.all_gather(jnp.stack(vectors).astype(F32), "fsdp", axis=1, tiled=True)
        b_up = lax.all_gather(bias_up.astype(F32), "fsdp", axis=0, tiled=True)
        b_up = b_up.reshape(SHARES, -1, FP).swapaxes(0, 1)
        b_up = b_up.reshape(b_up.shape[0], 1, -1)
        w_up = w_up.reshape(width, SHARES, -1, FP).transpose(2, 0, 1, 3).reshape(-1, width, SHARES * FP)
        w_down = w_down.reshape(SHARES, -1, FP, width).swapaxes(0, 1).reshape(-1, SHARES * FP, width)
    b_query, b_value, g_attn, s_attn = (vecs[i] for i in (0, 1, 3, 4))

    if not direct:
        normal_one, inverse_one = norm_stats(tokens)
        first_own = (normal_one * g_attn + s_attn).astype(BF16)
        first = order(first_own, swap(first_own), 1)
        joined = project(first, w_qkv)
        query = (joined[..., :half] + columns(b_query, 0, ctx)).astype(BF16)
        key = joined[..., half : 2 * half].astype(BF16)
        value = (joined[..., 2 * half :] + columns(b_value, 0, ctx)).astype(BF16)
        mixed_heads, lse = attention_forward(query, key, value, factor, size)

    def my_rows(x):
        return lax.dynamic_slice_in_dim(x, ctx * rows, rows, 1)

    def their_rows(x):
        return lax.dynamic_slice_in_dim(x, (1 - ctx) * rows, rows, 1)

    if not direct:
        mixed = order(my_rows(mixed_heads), swap(their_rows(mixed_heads)), 2)
    flat = (-1, width)
    d_out = cotangent.reshape(flat)
    result, d_middle, d_mixed, g_wmix, g_wup, g_wdown, gvec, *finished = middle_block(
        inputs.reshape(flat),
        mixed.reshape(flat),
        d_out,
        w_mix,
        w_up,
        w_down,
        vecs,
        b_up,
        SHARES,
        reps,
        direct,
    )
    steps = b_up.shape[0]
    if direct:
        d_tokens, summed, outs = backward_block(
            qkv, lse, inputs[:, 0], vecs, gvec, d_middle.reshape(tokens.shape), d_mixed.reshape(tokens.shape),
            first_t, w_qkv, [g_wdown, g_wup, g_wmix[None]], finished, owners, reps, factor, size,
        )
        o_wdown, o_wup, o_wmix, o_wqkv = (
            o.reshape(-1, n).astype(F32) for o, n in zip(outs, (width, SHARES * steps * FP, width, 3 * width))
        )
    else:
        d_mixed = d_mixed.reshape(tokens.shape)
        d_middle = d_middle.reshape(tokens.shape)
        d_heads = order(columns(d_mixed, 2, ctx), swap(columns(d_mixed, 2, 1 - ctx)), 1)
        d_query, d_key, d_value = attention_backward(query, key, value, d_heads, lse, factor, size)
        d_joined = jnp.concatenate([d_query, d_key, d_value], axis=-1)
        g_wqkv = outer_sum(first, d_joined)
        d_first = project_back(d_joined, w_qkv)
        d_first = my_rows(d_first) + swap(their_rows(d_first).astype(BF16)).astype(F32)
        normal_one, inverse_one = norm_stats(tokens)
        d_tokens = d_middle + norm_back(d_first, normal_one, inverse_one, g_attn)

        def reduce(grad):
            piece = lax.psum_scatter(
                grad.astype(BF16), ("fsdp", "rep", "ctx"), scatter_dimension=0, tiled=True
            )
            return lax.all_gather(piece, ("rep", "ctx"), axis=0, tiled=True).astype(F32)

        g_wdown = jnp.concatenate([g_wdown[f].reshape(SHARES, FP, width) for f in range(steps)], axis=1)
        o_wdown = reduce(g_wdown.reshape(-1, width))
        g_wup = jnp.stack([g_wup[f].reshape(width, SHARES, FP) for f in range(steps)], axis=2)
        o_wup = reduce(g_wup.reshape(width, -1))
        o_wmix = reduce(g_wmix.reshape(width, width))
        piece = lax.psum_scatter(g_wqkv.astype(BF16), ("fsdp", "rep"), scatter_dimension=0, tiled=True)
        piece = lax.all_gather(piece, "rep", axis=0, tiled=True)
        other = swap(piece)
        low, high = jnp.where(ctx == 0, piece, other), jnp.where(ctx == 0, other, piece)
        o_wqkv = jnp.concatenate(
            [t for i in range(3) for t in (low[:, i * half : (i + 1) * half], high[:, i * half : (i + 1) * half])],
            axis=1,
        ).astype(F32)

        def place(v):
            return lax.dynamic_update_slice_in_dim(jnp.zeros((width,), F32), v, ctx * half, 0)

        first_rows = (
            place(jnp.sum(d_query.astype(F32), axis=(0, 1))),
            place(jnp.sum(d_value.astype(F32), axis=(0, 1))),
            jnp.sum(d_first * normal_one, axis=(0, 1)),
            jnp.sum(d_first, axis=(0, 1)),
        )
        summed = jnp.concatenate([jnp.stack(first_rows[:2]), gvec[2:3], jnp.stack(first_rows[2:]), gvec[5:12]], axis=0)
        summed = lax.psum(summed, ("rep", "fsdp", "ctx"))
    owner = lax.axis_index("fsdp")
    o_bup = lax.dynamic_slice_in_dim(summed[8 : 8 + SHARES].reshape(-1), owner * b_up_rows, b_up_rows, 0)
    summed = lax.dynamic_slice_in_dim(summed[:8], owner * own, own, 1)
    o_bq, o_bv, o_bmix, o_ga, o_sa, o_gm, o_sm, o_bd = (summed[i] for i in range(8))
    return (
        result.reshape(inputs.shape),
        d_tokens[:, None],
        o_wqkv,
        o_bq,
        o_bv,
        o_wmix,
        o_bmix,
        o_ga,
        o_sa,
        o_gm,
        o_sm,
        o_wup,
        o_bup,
        o_wdown,
        o_bd,
    )


def solution(mesh):
    row = P(None, ("rep", "fsdp"), "ctx", None)
    mat = P("fsdp", None)
    vec = P("fsdp")
    params = (mat, vec, vec, mat, vec, vec, vec, vec, vec, mat, vec, mat, vec)
    in_specs = (row,) + params + (row,)
    out_specs = (row, row) + params
    return jax.shard_map(local, mesh=mesh, in_specs=in_specs, out_specs=out_specs, check_vma=False)
```

profile of v0, /device:TPU:1, one launch (start us, length us, event | category | flops | bytes accessed | tf_op | source)
XLA Modules:
  0.0 246.0 jit_solution(1629643109165581575)
XLA Ops:
  0.7 66.0 %forward_block.1 = (bf16[2,512,768]{2,1,0:T(8,128)(2,1)}, bf16[2,9,1024,128]{3,2,1,0:T(8,128)(2,1)}, bf16[768,2048]{1,0:T(8,128)(2,1)}, bf16[4,4,48,1152]{3,2,1,...) custom-call(bf16[2,512,768]{2,1,0:T(8,128)(2,1)} %bitcast.37, ...), custom_call_target="tpu_custom_call" | custom-call | tf_op jit(solution)/shard_map/forward_block/pallas_call | solution.py:572
  66.7 0.8 slice.33
  67.4 0.6 reshape.84.refs_7_
  68.0 69.4 %middle_block.1 = (bf16[1024,768]{1,0:T(8,128)(2,1)}, f32[1024,768]{1,0:T(8,128)}, bf16[1024,768]{1,0:T(8,128)(2,1)}, bf16[4,2,4,24,768]{4,3,2,1,0:T(8,128)(2,1)...) custom-call(bf16[1024,768]{1,0:T(8,128)(2,1)} %bitcast.38, ...), custom_call_target="tpu_custom_call" | custom-call | flops 32614907904 | bytes 31457280 | tf_op jit(solution)/shard_map/middle_block/pallas_call | solution.py:988
  137.4 96.0 %backward_block.1 = (f32[2,512,768]{2,1,0:T(8,128)}, f32[16,768]{1,0:T(8,128)}, bf16[3,2,4,32,768]{4,3,2,1,0:T(8,128)(2,1)}, bf16[2,4,24,3072]{3,2,1,0:T(8,128)(...) custom-call(bf16[2,9,1024,128]{3,2,1,0:T(8,128)(2,1)} %get-tuple-ele, ...), custom_call_target="tpu_custom_call", output_to_operand_aliasing={{2}: (14, {}), {3}: (15, {})} | custom-call | tf_op jit(solution)/shard_map/backward_block/pallas_call | solution.py:1296
  233.4 0.0 copy-start
  233.4 2.9 %bitcast_convert_fusion = f32[768,768]{1,0:T(8,128)} fusion(bf16[3,2,4,32,768]{4,3,2,1,0:T(8,128)(2,1)} %get-tuple-element.64), kind=kLoop, calls=%fused_computation | loop fusion | flops 589824 | bytes 3538944 | tf_op jit(solution)/shard_map/convert_element_type | solution.py:1454
  236.3 0.0 copy-done
  236.3 0.0 copy-start.2
  236.3 1.7 bitcast_convert_fusion.1
  238.1 0.0 copy-start.3
  238.1 0.0 copy-done.2
  238.1 0.0 copy-start.4
  238.1 1.4 bitcast_convert_fusion.2
  239.5 0.0 copy-done.3
  239.5 0.9 bitcast_convert_fusion.3
  240.3 0.0 copy-start.1
  240.3 0.0 copy-done.4
  240.3 0.7 fusion
  241.0 0.7 dynamic_slice.7
  241.7 2.7 %copy.38 = bf16[2,1,512,768]{3,2,1,0:T(8,128)(2,1)} copy(bf16[2,1,512,768]{3,2,1,0:T(8,128)(2,1)} %bitcast.44) | data formatting | bytes 3145728
  244.4 0.0 copy-done.1
  244.4 1.7 copy.39
  (3 shorter events, 0.0 us)
Async XLA Ops:
  233.4 3.0 %copy-start = (bf16[2,4,24,3072]{3,2,1,0:T(8,128)(2,1)S(1)}, bf16[2,4,24,3072]{3,2,1,0:T(8,128)(2,1)}, u32[]{:S(2)}) copy-start(bf16[2,4,24,3072]{3,2,1,0:T(8,128)(2,1)} %get-tuple-element.63) | copy-start | bytes 3538948
  236.3 1.7 copy-start.2
  238.1 1.4 copy-start.3
  238.1 2.3 copy-start.4
  240.3 4.0 %copy-start.1 = (f32[2,512,768]{2,1,0:T(8,128)S(1)}, f32[2,512,768]{2,1,0:T(8,128)}, u32[]{:S(2)}) copy-start(f32[2,512,768]{2,1,0:T(8,128)} %get-tuple-element.59) | copy-start | bytes 9437188
where the time goes:
time: 249 us; the launch traced here: 246 us
  Pallas kernels  231 us (93%)
  local copies, waits for them, and re-layouts  7.07 us (3%)
  other arithmetic  6.93 us (3%)
    pallas_call x1, Pallas kernels, backward_block(): pl.pallas_call(partial(backward_kernel, owners, reps, pairs, factor, size...  96 us
    pallas_call x1, Pallas kernels, middle_block(): pl.pallas_call(partial(middle_kernel, owners, reps, direct), grid=(steps,...  69.4 us
    pallas_call x1, Pallas kernels, forward_block(): pl.pallas_call(partial(forward_kernel, owners, reps, pairs, factor, size)...  66 us
    convert_element_type x4, other arithmetic, local(): o.reshape(-1, n).astype(F32)  6.93 us

commit v1 on v0

--- a/solution.py
+++ b/solution.py
@@ -13,6 +13,7 @@
 F32 = jnp.float32
 QB = 256
 TB = 256
+RB = 512
 FP = 256
 SHARES = 4
 GELU_A = 0.7978845608028654
@@ -194,12 +195,14 @@
     return lax.axis_index("fsdp"), lax.axis_index("rep"), lax.axis_index("ctx")
 
 
-def greet(owners, reps):
+def greet(owners, reps, across=False):
     z, r, c = position()
     barrier = pltpu.get_barrier_semaphore()
     peers = [{"fsdp": lax.rem(z + j, owners)} for j in range(1, owners)]
     peers += [{"rep": r ^ j} for j in range(1, reps)]
     peers += [{"ctx": 1 - c}]
+    if across:
+        peers += [{"rep": r ^ j, "ctx": 1 - c} for j in range(1, reps)]
     for peer in peers:
         pl.semaphore_signal(barrier, inc=1, device_id=peer, device_id_type=MESH)
     pl.semaphore_wait(barrier, len(peers))
@@ -701,22 +704,21 @@
 def timetable(groups, products):
     table = []
     for g in range(groups):
-        second = 6 + 4 * g
-        times = (1 + 2 * g, second, second + 5, second + 9, second + 11, second + 13, second + 15)
+        second = 4 + 5 * g
+        times = (2 * g - 1, second, second + 5, second + 9, second + 11, second + 13, second + 15)
         table += [(t, g, 1 + i) for i, t in enumerate(times)]
-    for p, second in zip(range(products), (20, 27, 28)):
+    for p, second in zip(range(products), (25, 27, 28)):
         times = (second, second + 4, second + 8, second + 10, second + 12, second + 14)
         table += [(t, groups + p, 2 + i) for i, t in enumerate(times)]
     return sorted(table)
 
 
 def gelu_parts(b):
-    square = b * b
-    inner = GELU_A * b * (1.0 + GELU_B * square)
-    t = jnp.tanh(inner)
-    rise = 0.5 * (1.0 + t)
-    slope = rise + 0.5 * b * (1.0 - t * t) * (GELU_A * (1.0 + 3.0 * GELU_B * square))
-    return b * rise, slope
+    cubic = (GELU_A * GELU_B) * (b * b)
+    t = jnp.tanh(b * (cubic + GELU_A))
+    rise = 0.5 * t + 0.5
+    active = b * rise
+    return active, rise + active * (1.0 - t) * (3.0 * cubic + GELU_A)
 
 
 GATHERS = [
@@ -732,18 +734,22 @@
 
 def middle_kernel(owners, reps, direct, *refs):
     x_ref, mixed_ref, d_ref, wmix_ref, wup_any, wdown_any, vec_ref, bup_ref = refs[:8]
-    result_ref, dmid_ref, dmixed_ref, gmix_ref, gup_ref, gdown_ref, gvec_ref = refs[8:15]
-    refs = refs[15:]
+    result_ref, dmid_ref, gmix_ref, gvec_ref = refs[8:12]
+    refs = refs[12:]
     if direct:
-        down_out, up_out, refs = refs[0], refs[1], refs[2:]
+        heads_out, up_sums, down_sums, down_out, up_out, dmixed_ref, gup_ref, gdown_ref, up_got, down_got = refs[:10]
+        refs = refs[10:]
+    else:
+        dmixed_ref, gup_ref, gdown_ref = refs[:3]
+        refs = refs[3:]
     middle, second, second_t, mixed_t, out_sum, ds_sum, active_t, d_before, w_up, w_down = refs[:10]
     refs = refs[10:]
     step = pl.program_id(0)
     rows = x_ref.shape[0]
     steps = w_up.shape[0]
     last = steps - 1
-    count = rows // TB
-    chunk = lambda i: pl.ds(pl.multiple_of(i * TB, TB), TB)
+    count = rows // RB
+    chunk = lambda i: pl.ds(pl.multiple_of(i * RB, RB), RB)
     b_mix, gain, shift, b_down = (vec_ref[i : i + 1, :] for i in (2, 5, 6, 7))
     slots = 4
 
@@ -786,6 +792,22 @@
                     row_halves,
                     lambda o, f=f, w=whole, of=of, side=side: side(of(w, f, o), c),
                 )
+        cores = []
+        for f in range(1, steps):
+            for tag, ref, got, sums in (("d", gdown_ref, down_got, down_sums), ("u", gup_ref, up_got, up_sums)):
+                there = lambda got=got, f=f: got.at[f - 1]
+                plan.add(("core", tag, f), lambda ref=ref: ref.at[0, :, 1 - c], there, {"ctx": 1 - c})
+                cores.append((f, ("core", tag, f), ref, there, local(there, lambda sums=sums, f=f: sums.at[f - 1])))
+        mbs, pairs, lanes = heads_out.shape[1], heads_out.shape[0], heads_out.shape[3]
+        seq = rows // mbs
+        seq_rows = pl.ds(pl.multiple_of(c * seq, seq), seq)
+        kept_heads = []
+        for m in range(mbs):
+            for p in range(pairs):
+                part_of = lambda side, m=m, p=p: dmixed_ref.at[pl.ds(m * seq, seq), slab(side * pairs + p, lanes)]
+                to = lambda m=m, p=p: heads_out.at[p, m, seq_rows]
+                plan.add(("heads", m, p), partial(part_of, 1 - c), to, {"ctx": 1 - c})
+                kept_heads.append(local(partial(part_of, c), to))
         flows, leaving, at = [], [], 0
         for i, (ref, out) in enumerate(((gdown_ref, down_out), (gup_ref, up_out))):
             wide = ref.shape[-1] // 2
@@ -821,6 +843,14 @@
             lambda: pltpu.make_async_copy(wdown_any, w_down, kept.at[1]),
         ]
 
+    def core_sums(step):
+        for f, name, ref, there, out in cores:
+            if f == step:
+                plan.arrive(name)
+                add_blocks(there(), [there(), ref.at[0, :, c]], BF16)
+                out().start()
+                plan.leave(name)
+
     def between(slot, here=True):
         if not direct:
             return
@@ -895,17 +925,31 @@
         def _():
             plan.leave(*[(flow.name, "core") for flow in flows])
 
+        @pl.when(step == 2)
+        def _():
+            core_sums(1)
+
     share = second_t.shape[0] // owners
     part = active_t.shape[0] // owners
 
     def weights(o, _):
-        lines = pl.ds(pl.multiple_of(o * part, part), part)
-        gdown_ref[0, o] = dot_nn(active_t[lines], d_ref[...]).reshape(gdown_ref.shape[2:]).astype(BF16)
-        lines = pl.ds(pl.multiple_of(o * share, 64), share)
-        gup_ref[0, o] = dot_nn(second_t[lines], d_before[...]).reshape(gup_ref.shape[2:]).astype(BF16)
+        two = pl.ds(2 * o, 2)
+        lines = pl.ds(pl.multiple_of(o * 2 * part, part), 2 * part)
+        gdown_ref[0, two] = dot_nn(active_t[lines], d_ref[...]).reshape((2,) + gdown_ref.shape[2:]).astype(BF16)
+        lines = pl.ds(pl.multiple_of(o * 2 * share, 64), 2 * share)
+        gup_ref[0, two] = dot_nn(second_t[lines], d_before[...]).reshape((2,) + gup_ref.shape[2:]).astype(BF16)
         return 0
 
-    lax.fori_loop(0, owners, weights, 0)
+    lax.fori_loop(0, owners // 2, weights, 0)
+    if direct:
+        for f in range(1, steps):
+
+            @pl.when(step == f)
+            def _():
+                for when, name, *_ in cores:
+                    if when == f:
+                        plan.start(name)
+
     between(slots - 1)
 
     @pl.when(step == last)
@@ -930,6 +974,11 @@
         for i, k in enumerate((2, 5, 6, 7)):
             gvec_ref[k : k + 1, :] = sums[i]
 
+        if direct:
+            plan.start(*[("heads", m, p) for m in range(mbs) for p in range(pairs)])
+            for copy in kept_heads:
+                copy().start()
+
         def mix(o, _):
             lines = pl.ds(pl.multiple_of(o * share, 64), share)
             gmix_ref[o] = dot_nn(mixed_t[lines], second[...]).reshape(gmix_ref.shape[1:]).astype(BF16)
@@ -937,16 +986,20 @@
 
         lax.fori_loop(0, owners, mix, 0)
         if direct:
+            core_sums(last)
             for when, g, n in SUMS:
                 if when >= steps * slots:
                     for flow in flows[2 * g : 2 * g + 2]:
                         flow.step(n)
+            plan.arrive(*[("heads", m, p) for m in range(mbs) for p in range(pairs)])
             plan.close()
+            for copy in kept_heads + [out for *_, out in cores]:
+                copy().wait()
             for copy in leaving:
                 copy().wait()
 
 
-def middle_block(x, mixed, d_out, w_mix, w_up, w_down, vecs, b_up, owners, reps, direct):
+def middle_block(x, mixed, d_out, w_mix, w_up, w_down, vecs, b_up, owners, reps, direct, heads):
     rows, width = x.shape
     steps = w_up.shape[0]
     ff = steps * owners * FP
@@ -956,11 +1009,8 @@
     vmem = pltpu.VMEM
     side = (owners, 2, reps)
     g_mix = side + (width // owners // 2 // reps, width)
-    given = steps - 1 if direct else steps
-    g_up = (given,) + g_mix[:-1] + (owners * FP,)
-    g_down = (given,) + side + (FP // 2 // reps, width)
-    skip = steps - given
-    per_step = lambda s: pl.BlockSpec((1,) + s[1:], lambda f: (jnp.maximum(f - skip, 0),) + (0,) * (len(s) - 1))
+    g_up = (1,) + g_mix[:-1] + (owners * FP,)
+    g_down = (1,) + side + (FP // 2 // reps, width)
     scratch = [
         vmem((rows, width), F32),
         vmem((rows, width), BF16),
@@ -973,16 +1023,25 @@
         vmem((steps, width, owners * FP), BF16),
         vmem((steps, owners * FP, width), BF16),
     ]
-    finished = []
+    grads = [vmem((rows, width), BF16), vmem(g_up, BF16), vmem(g_down, BF16)]
     if direct:
-        finished = [out((steps,) + g_down[2:], BF16), out(g_up[2:5] + (steps * g_up[5],), BF16)]
+        later = [(steps - 1, g[1]) + g[3:] for g in (g_up, g_down)]
+        extra = [out(heads, BF16)] + [out(s, BF16) for s in later]
+        extra += [out((steps,) + g_down[2:], BF16), out(g_up[2:5] + (steps * g_up[5],), BF16)]
+        extra_specs = [anywhere] * 5
+        scratch = grads + [vmem(s, BF16) for s in later] + scratch
         for g in (g_down, g_up):
             for _ in range(2):
                 scratch += flow_scratch(owners, reps, (g[4], g[5] // 2), True)
-        remotes = (steps - 1) * 2 * 15 + 4 * 11
-        scratch += [pltpu.SemaphoreType.DMA((remotes,))] * 2 + [pltpu.SemaphoreType.DMA((2 * owners + 2 * (steps - 1) * owners + 10,))]
+        remotes = (steps - 1) * 2 * 15 + 4 * 11 + 2 * (steps - 1) + heads[0] * heads[1]
+        scratch += [pltpu.SemaphoreType.DMA((remotes,))] * 2 + [
+            pltpu.SemaphoreType.DMA((2 * owners + 2 * (steps - 1) * owners + 10 + 2 * (steps - 1) + heads[0] * heads[1],))
+        ]
         params = dict(collective_id=3, has_side_effects=True)
     else:
+        per_step = lambda s: pl.BlockSpec(s, lambda f: (f,) + (0,) * (len(s) - 1))
+        extra = [out((rows, width), BF16)] + [out((steps,) + g[1:], BF16) for g in (g_up, g_down)]
+        extra_specs = [whole((rows, width)), per_step(g_up), per_step(g_down)]
         scratch += [pltpu.SemaphoreType.DMA((2,))]
         params = {}
     return pl.pallas_call(
@@ -990,26 +1049,8 @@
         grid=(steps,),
         in_specs=[whole((rows, width))] * 3
         + [whole((width, width)), anywhere, anywhere, whole(vecs.shape), pl.BlockSpec((1, 1, owners * FP), lambda f: (f, 0, 0))],
-        out_specs=[
-            whole((rows, width)),
-            whole((rows, width)),
-            whole((rows, width)),
-            whole(g_mix),
-            per_step(g_up),
-            per_step(g_down),
-            whole((16, width)),
-        ]
-        + [anywhere] * len(finished),
-        out_shape=[
-            out((rows, width), BF16),
-            out((rows, width), F32),
-            out((rows, width), BF16),
-            out(g_mix, BF16),
-            out(g_up, BF16),
-            out(g_down, BF16),
-            out((16, width), F32),
-        ]
-        + finished,
+        out_specs=[whole((rows, width)), whole((rows, width)), whole(g_mix), whole((16, width))] + extra_specs,
+        out_shape=[out((rows, width), BF16), out((rows, width), F32), out(g_mix, BF16), out((16, width), F32)] + extra,
         scratch_shapes=scratch,
         compiler_params=pltpu.CompilerParams(vmem_limit_bytes=62 << 20, **params),
         cost_estimate=pl.CostEstimate(
@@ -1023,14 +1064,14 @@
 
 def backward_kernel(
     owners, reps, pairs, factor, size, shapes, done,
-    q_ref, k_ref, v_ref, lse_ref, x_ref, vec_ref, gvec_ref, dmid_ref, dmixed_ref, first_t_ref, w_ref, *refs
+    q_ref, k_ref, v_ref, d_heads, lse_ref, x_ref, vec_ref, gvec_ref, dmid_ref, first_t_ref, w_ref, *refs
 ):
     n_in = len(shapes)
     sources, refs = refs[:n_in], refs[n_in + 2 :]
     dtok_ref, vec_out, refs = refs[0], refs[1], refs[2:]
     outs, refs = refs[: n_in + 1], refs[n_in + 1 :]
-    d_heads, d_joined, first_t, w_pairs, df_send, df_recv, dk_sum, dv_sum, b_sum, vec_one, vec_got, vec_sum, refs = (
-        refs[:12] + (refs[12:],)
+    d_joined, first_t, w_pairs, df_send, df_recv, dk_sum, dv_sum, b_sum, vec_one, vec_got, vec_sum, refs = (
+        refs[:11] + (refs[11:],)
     )
     flow_refs, (send, recv, kept) = refs[:-3], refs[-3:]
     step = pl.program_id(0)
@@ -1065,8 +1106,10 @@
         for f in range(shape[0]):
             wide = shape[-1] // 2
             for s in range(2):
-                mine, theirs, *hops = flow_refs[at : at + 6]
-                at += 6
+                split = len(shape) == 6
+                mine, *hops = flow_refs[at : at + 5 + split]
+                at += 5 + split
+                theirs = hops.pop(0) if split else None
                 source, out, cols = sources[i], outs[i], pl.ds(s * wide, wide)
                 if i == 1:
                     places = []
@@ -1081,8 +1124,13 @@
                     places = [(lambda final: final, lambda out=out, f=f + skip, cols=cols: out.at[f, :, :, :, cols])]
                 add_flow(
                     (i, f, s), (1, 2) if s == 0 else (2, 1), mine, theirs, hops, places,
-                    local(lambda source=source, f=f, cols=cols: source.at[f, :, c, :, :, cols], lambda mine=mine: mine),
-                    lambda source=source, f=f, cols=cols: source.at[f, :, 1 - c, :, :, cols],
+                    local(
+                        lambda source=source, f=f, cols=cols, split=split: (
+                            source.at[f, :, c, :, :, cols] if split else source.at[f, :, :, :, cols]
+                        ),
+                        lambda mine=mine: mine,
+                    ),
+                    (lambda source=source, f=f, cols=cols: source.at[f, :, 1 - c, :, :, cols]) if split else None,
                 )
     for p in range(pairs):
         for s in range(2):
@@ -1107,57 +1155,43 @@
             flow.step(stage)
 
     for m in range(mbs):
-        for p in range(pairs):
-            plan.add(
-                ("heads", m, p),
-                lambda m=m, p=p: dmixed_ref.at[m, :, slab((1 - c) * pairs + p, lanes)],
-                lambda m=m, p=p: d_heads.at[p, m, own_rows],
-                {"ctx": 1 - c},
-            )
         plan.add(("first", m), lambda m=m: df_send.at[m], lambda m=m: df_recv.at[m], {"ctx": 1 - c})
-    for i, peer in enumerate([{"ctx": 1 - c}, {"rep": r ^ 1}, {"rep": r ^ 2}]):
-        plan.add(("vec", i), lambda i=i: vec_sum.at[i], lambda i=i: vec_got.at[i], peer)
+    around = [(k, side) for k in range(reps) for side in range(2) if k or side]
+    for k, side in around:
+        peer = {"rep": r ^ k, "ctx": 1 - c if side else c}
+        plan.add(("vec", k, side), lambda: vec_sum.at[0], lambda k=k, side=side: vec_got.at[2 * k + side], peer)
     for j in range(1, owners):
         plan.add(
-            ("vec", "z", j), lambda: vec_sum.at[3], lambda j=j: vec_got.at[2 + j], {"fsdp": lax.rem(z + j, owners)}
+            ("vec", "z", j), lambda: vec_sum.at[1], lambda j=j: vec_got.at[2 * reps + j - 1], {"fsdp": lax.rem(z + j, owners)}
         )
 
-    def own_heads(m, p):
-        return pltpu.make_async_copy(
-            dmixed_ref.at[m, :, slab(c * pairs + p, lanes)], d_heads.at[p, m, own_rows], kept.at[locals_used + m * pairs + p]
-        )
+    table = timetable(products, pairs)
+    quarters = 2 * rows // QB
+    tail = [entry for entry in table if entry[0] >= quarters * mbs * pairs]
 
     def load_first():
-        return pltpu.make_async_copy(first_t_ref, first_t, kept.at[locals_used + mbs * pairs])
+        return pltpu.make_async_copy(first_t_ref, first_t, kept.at[locals_used])
 
     def load_weight(i, p):
         return pltpu.make_async_copy(
             w_ref.at[:, pl.ds((i * pairs + p) * lanes, lanes)],
             w_pairs.at[p, :, pl.ds(i * lanes, lanes)],
-            kept.at[locals_used + mbs * pairs + 1 + i * pairs + p],
+            kept.at[locals_used + 1 + i * pairs + p],
         )
 
     @pl.when(step == 0)
     def _():
-        greet(owners, reps)
-        for p in range(pairs):
-            for m in range(mbs):
-                plan.start(("heads", m, p))
-                own_heads(m, p).start()
+        greet(owners, reps, across=True)
         for g in range(products):
             advance(g, 0)
         load_first().start()
         for i in range(3):
             for p in range(pairs):
                 load_weight(i, p).start()
-        for p in range(pairs):
-            for m in range(mbs):
-                plan.arrive(("heads", m, p))
-                own_heads(m, p).wait()
-
-    table = timetable(products, pairs)
-    quarters = 2 * rows // QB
-    tail = [entry for entry in table if entry[0] >= quarters * mbs * pairs]
+        for when, group, stage in table:
+            if when < 0:
+                advance(group, stage)
+
 
     def between(k, done):
         for i in range(mbs * pairs):
@@ -1191,7 +1225,7 @@
         start = pl.multiple_of(m * 2 * rows, 2 * rows)
         joined = d_joined.at[p, pl.ds(start, 2 * rows)]
         attention_backward_block(
-            factor, size, q_ref.at[0, 0], k_ref.at[0, 0], v_ref.at[0, 0], d_heads.at[p, m], lse_ref.at[m, p],
+            factor, size, q_ref.at[0, 0], k_ref.at[0, 0], v_ref.at[0, 0], d_heads.at[0, 0], lse_ref.at[m, p],
             joined.at[:, pl.ds(0, lanes)], joined.at[:, pl.ds(lanes, lanes)], joined.at[:, pl.ds(2 * lanes, lanes)],
             dk_sum, dv_sum, partial(between, step),
         )
@@ -1250,17 +1284,17 @@
             for i in range(2):
                 vec_one[i : i + 1, slab(c * pairs + p, lanes)] = b_sum[p, i : i + 1, :]
         vec_sum[0] = vec_one[...]
-        plan.start(("vec", 0))
-        for i in range(3):
-            go(36 + 2 * i)
-            plan.arrive(("vec", i))
-            vec_sum[i + 1] = vec_sum[i] + vec_got[i]
-            if i < 2:
-                plan.start(("vec", i + 1))
+        plan.start(*[("vec", k, side) for k, side in around])
+        go(37)
+        plan.arrive(*[("vec", k, side) for k, side in around])
+        vec_got[0] = vec_one[...]
+        cores = [vec_got[2 * k] + vec_got[2 * k + 1] for k in range(reps)]
+        vec_sum[1] = (cores[0] + cores[1]) + (cores[2] + cores[3])
         plan.start(*[("vec", "z", j) for j in range(1, owners)])
-        go(42)
+        go(41)
         plan.arrive(*[("vec", "z", j) for j in range(1, owners)])
-        vec_out[...] = (vec_sum[3] + vec_got[3]) + (vec_got[4] + vec_got[5])
+        n = 2 * reps
+        vec_out[...] = (vec_sum[1] + vec_got[n]) + (vec_got[n + 1] + vec_got[n + 2])
         go(1000)
         plan.close()
         for copy in leaving:
@@ -1268,7 +1302,7 @@
 
 
 def backward_block(
-    qkv, lse, x, vecs, gvec, d_middle, d_mixed, first_t, w_qkv, grads, finished, owners, reps, factor, size
+    qkv, heads, lse, x, vecs, gvec, d_middle, first_t, w_qkv, grads, finished, owners, reps, factor, size
 ):
     mbs, rows, width = x.shape
     lanes = 2 * size
@@ -1285,24 +1319,29 @@
 
         return pl.BlockSpec((1, 1, 2 * rows, lanes), index)
 
-    pieces = [(g.shape[4], g.shape[5] // 2) for g in grads for _ in range(2 * g.shape[0])]
+    def heads_index(i):
+        k = jnp.minimum(i, final_step)
+        return (lax.div(k, mbs), lax.rem(k, mbs), 0, 0)
+
+    heads_spec = pl.BlockSpec((1, 1, 2 * rows, lanes), heads_index)
+    pieces = [(len(g.shape) == 6, (g.shape[-2], g.shape[-1] // 2)) for g in grads for _ in range(2 * g.shape[0])]
     q_piece = (width // owners // reps // 2, 3 * lanes)
     down, up, mix = (g.shape for g in grads)
     finals = [f.shape for f in finished] + [mix[:1] + mix[2:], (reps, 2, q_piece[0], 3 * width)]
-    scratch = [s for p in pieces for s in flow_scratch(owners, reps, p, True)]
+    scratch = [s for split, p in pieces for s in flow_scratch(owners, reps, p, split)]
     scratch += [s for _ in range(2 * pairs) for s in flow_scratch(owners, reps, q_piece, False)]
-    remotes = 11 * len(pieces) + 10 * 2 * pairs + mbs * pairs + mbs + 6
+    remotes = 11 * len(pieces) + 10 * 2 * pairs + mbs * pairs + mbs + 2 * reps + owners
     vec = (16, width)
     dtok, vec_sum, *outs = pl.pallas_call(
         partial(backward_kernel, owners, reps, pairs, factor, size, [g.shape for g in grads], finished[0].shape[0] - down[0]),
         grid=(mbs * pairs + 1,),
-        in_specs=[block(0), block(1), block(2), whole(lse.shape), whole(x.shape), whole(vec), whole(vec), whole(x.shape)]
-        + [anywhere] * (3 + len(grads) + 2),
+        in_specs=[block(0), block(1), block(2), heads_spec, whole(lse.shape), whole(x.shape), whole(vec), whole(vec)]
+        + [whole(x.shape)]
+        + [anywhere] * (2 + len(grads) + 2),
         input_output_aliases={11 + len(grads): 2, 12 + len(grads): 3},
         out_specs=[whole(x.shape), whole(vec)] + [anywhere] * len(finals),
         out_shape=[shape(x.shape, F32), shape(vec, F32)] + [shape(f, BF16) for f in finals],
         scratch_shapes=[
-            pltpu.VMEM((pairs, mbs, 2 * rows, lanes), BF16),
             pltpu.VMEM((pairs, mbs * 2 * rows, 3 * lanes), BF16),
             pltpu.VMEM(first_t.shape, BF16),
             pltpu.VMEM((pairs, width, 3 * lanes), BF16),
@@ -1312,8 +1351,8 @@
             pltpu.VMEM((2 * rows, lanes), F32),
             pltpu.VMEM((pairs, 8, lanes), F32),
             pltpu.VMEM(vec, F32),
-            pltpu.VMEM((6,) + vec, F32),
-            pltpu.VMEM((4,) + vec, F32),
+            pltpu.VMEM((2 * reps + owners - 1,) + vec, F32),
+            pltpu.VMEM((2,) + vec, F32),
         ]
         + scratch
         + [
@@ -1325,7 +1364,7 @@
             collective_id=2, has_side_effects=True, vmem_limit_bytes=63 << 20
         ),
         name="backward_block",
-    )(qkv, qkv, qkv, lse, x, vecs, gvec, d_middle, d_mixed, first_t, w_qkv, *grads, *finished)
+    )(qkv, qkv, qkv, heads, lse, x, vecs, gvec, d_middle, first_t, w_qkv, *grads, *finished)
     return dtok, vec_sum, outs
 
 
@@ -1431,7 +1470,7 @@
         mixed = order(my_rows(mixed_heads), swap(their_rows(mixed_heads)), 2)
     flat = (-1, width)
     d_out = cotangent.reshape(flat)
-    result, d_middle, d_mixed, g_wmix, g_wup, g_wdown, gvec, *finished = middle_block(
+    result, d_middle, g_wmix, gvec, d_mixed, g_wup, g_wdown, *finished = middle_block(
         inputs.reshape(flat),
         mixed.reshape(flat),
         d_out,
@@ -1443,12 +1482,12 @@
         SHARES,
         reps,
         direct,
+        (half // (2 * size), inputs.shape[0], 2 * rows, 2 * size),
     )
     steps = b_up.shape[0]
     if direct:
         d_tokens, summed, outs = backward_block(
-            qkv, lse, inputs[:, 0], vecs, gvec, d_middle.reshape(tokens.shape), d_mixed.reshape(tokens.shape),
-            first_t, w_qkv, [g_wdown, g_wup, g_wmix[None]], finished, owners, reps, factor, size,
+            qkv, d_mixed, lse, inputs[:, 0], vecs, gvec, d_middle.reshape(tokens.shape), first_t, w_qkv, [g_wdown, g_wup, g_wmix[None]], finished, owners, reps, factor, size,
         )
         o_wdown, o_wup, o_wmix, o_wqkv = (
             o.reshape(-1, n).astype(F32) for o, n in zip(outs, (width, SHARES * steps * FP, width, 3 * width))

time: 249 us -> 243 us (0.976)
  Pallas kernels: 231 us -> 228 us
where the time goes in v1:
time: 243 us; the launch traced here: 242 us
  Pallas kernels  228 us (94%)
  other arithmetic  6.94 us (3%)
  local copies, waits for them, and re-layouts  6.87 us (3%)
    pallas_call x1, Pallas kernels, backward_block(): pl.pallas_call(partial(backward_kernel, owners, reps, pairs, factor, size...  93.6 us
    pallas_call x1, Pallas kernels, middle_block(): pl.pallas_call(partial(middle_kernel, owners, reps, direct), grid=(steps,...  68.4 us
    pallas_call x1, Pallas kernels, forward_block(): pl.pallas_call(partial(forward_kernel, owners, reps, pairs, factor, size)...  66 us
    convert_element_type x4, other arithmetic, local(): o.reshape(-1, n).astype(F32)  6.94 us

profile of v1, /device:TPU:1, one launch (start us, length us, event | category | flops | bytes accessed | tf_op | source)
XLA Modules:
  0.0 242.4 jit_solution(16274685659086151232)
XLA Ops:
  0.7 66.0 %forward_block.1 = (bf16[2,512,768]{2,1,0:T(8,128)(2,1)}, bf16[2,9,1024,128]{3,2,1,0:T(8,128)(2,1)}, bf16[768,2048]{1,0:T(8,128)(2,1)}, bf16[4,4,48,1152]{3,2,1,...) custom-call(bf16[2,512,768]{2,1,0:T(8,128)(2,1)} %bitcast.36, ...), custom_call_target="tpu_custom_call" | custom-call | tf_op jit(solution)/shard_map/forward_block/pallas_call | solution.py:575
  66.6 0.8 slice.33
  67.4 0.6 reshape.81.refs_7_
  68.0 68.4 %middle_block.1 = (bf16[1024,768]{1,0:T(8,128)(2,1)}, f32[1024,768]{1,0:T(8,128)}, bf16[4,2,4,24,768]{4,3,2,1,0:T(8,128)(2,1)}, f32[16,768]{1,0:T(8,128)}, bf16[...) custom-call(bf16[1024,768]{1,0:T(8,128)(2,1)} %bitcast.37, ...), custom_call_target="tpu_custom_call" | custom-call | flops 32614907904 | bytes 31457280 | tf_op jit(solution)/shard_map/middle_block/pallas_call | solution.py:1047
  136.4 93.6 %backward_block.1 = (f32[2,512,768]{2,1,0:T(8,128)}, f32[16,768]{1,0:T(8,128)}, bf16[3,2,4,32,768]{4,3,2,1,0:T(8,128)(2,1)}, bf16[2,4,24,3072]{3,2,1,0:T(8,128)(...) custom-call(bf16[2,9,1024,128]{3,2,1,0:T(8,128)(2,1)} %get-tuple-ele, ...), custom_call_target="tpu_custom_call", output_to_operand_aliasing={{2}: (14, {}), {3}: (15, {})} | custom-call | tf_op jit(solution)/shard_map/backward_block/pallas_call | solution.py:1335
  230.0 0.0 copy-start
  230.0 2.9 %bitcast_convert_fusion = f32[768,768]{1,0:T(8,128)} fusion(bf16[3,2,4,32,768]{4,3,2,1,0:T(8,128)(2,1)} %get-tuple-element.64), kind=kLoop, calls=%fused_computation | loop fusion | flops 589824 | bytes 3538944 | tf_op jit(solution)/shard_map/convert_element_type | solution.py:1493
  232.9 0.0 copy-done
  232.9 0.0 copy-start.3
  232.9 1.7 bitcast_convert_fusion.1
  234.7 0.0 copy-start.4
  234.7 0.0 copy-done.3
  234.7 0.0 copy-start.5
  234.7 0.0 copy-start.2
  234.7 1.4 bitcast_convert_fusion.2
  236.1 0.0 copy-done.4
  236.1 0.9 bitcast_convert_fusion.3
  236.9 0.0 copy-done.5
  236.9 0.7 fusion
  237.6 0.7 dynamic_slice.7
  238.3 0.0 copy-done.2
  238.3 0.0 copy-start.1
  238.3 1.1 copy.38
  239.5 1.3 copy-done.1
  240.8 1.7 copy.39
  (3 shorter events, 0.0 us)
Async XLA Ops:
  230.0 3.0 %copy-start = (bf16[2,4,24,3072]{3,2,1,0:T(8,128)(2,1)S(1)}, bf16[2,4,24,3072]{3,2,1,0:T(8,128)(2,1)}, u32[]{:S(2)}) copy-start(bf16[2,4,24,3072]{3,2,1,0:T(8,128)(2,1)} %get-tuple-element.63) | copy-start | bytes 3538948
  232.9 1.7 copy-start.3
  234.7 1.4 copy-start.4
  234.7 2.3 copy-start.5
  234.7 3.6 %copy-start.2 = (bf16[1024,768]{1,0:T(8,128)(2,1)S(1)}, bf16[1024,768]{1,0:T(8,128)(2,1)}, u32[]{:S(2)}) copy-start(bf16[1024,768]{1,0:T(8,128)(2,1)} %get-tuple-element.46) | copy-start | bytes 4718596
  238.3 2.5 %copy-start.1 = (f32[2,512,768]{2,1,0:T(8,128)S(1)}, f32[2,512,768]{2,1,0:T(8,128)}, u32[]{:S(2)}) copy-start(f32[2,512,768]{2,1,0:T(8,128)} %get-tuple-element.59) | copy-start | bytes 9437188

commit v2 on v1

--- a/solution.py
+++ b/solution.py
@@ -1181,13 +1181,17 @@
 
     @pl.when(step == 0)
     def _():
-        greet(owners, reps, across=True)
-        for g in range(products):
+        within = [g for g in range(products) if not groups[g][0].split]
+        for g in within:
             advance(g, 0)
         load_first().start()
         for i in range(3):
             for p in range(pairs):
                 load_weight(i, p).start()
+        greet(owners, reps, across=True)
+        for g in range(products):
+            if g not in within:
+                advance(g, 0)
         for when, group, stage in table:
             if when < 0:
                 advance(group, stage)

time: 243 us -> 242 us (level)
  no operation moved by 1% of the time
where the time goes in v2:
time: 242 us; the launch traced here: 241 us
  Pallas kernels  227 us (94%)
  other arithmetic  6.94 us (3%)
  local copies, waits for them, and re-layouts  6.87 us (3%)
    pallas_call x1, Pallas kernels, backward_block(): pl.pallas_call(partial(backward_kernel, owners, reps, pairs, factor, size...  92.5 us
    pallas_call x1, Pallas kernels, middle_block(): pl.pallas_call(partial(middle_kernel, owners, reps, direct), grid=(steps,...  68.4 us
    pallas_call x1, Pallas kernels, forward_block(): pl.pallas_call(partial(forward_kernel, owners, reps, pairs, factor, size)...  66 us
    convert_element_type x4, other arithmetic, local(): o.reshape(-1, n).astype(F32)  6.94 us

profile of v2, /device:TPU:1, one launch (start us, length us, event | category | flops | bytes accessed | tf_op | source)
XLA Modules:
  0.0 241.4 jit_solution(10240928559155759728)
XLA Ops:
  0.7 66.0 %forward_block.1 = (bf16[2,512,768]{2,1,0:T(8,128)(2,1)}, bf16[2,9,1024,128]{3,2,1,0:T(8,128)(2,1)}, bf16[768,2048]{1,0:T(8,128)(2,1)}, bf16[4,4,48,1152]{3,2,1,...) custom-call(bf16[2,512,768]{2,1,0:T(8,128)(2,1)} %bitcast.36, ...), custom_call_target="tpu_custom_call" | custom-call | tf_op jit(solution)/shard_map/forward_block/pallas_call | solution.py:575
  66.6 0.8 slice.33
  67.4 0.6 reshape.81.refs_7_
  68.0 68.4 %middle_block.1 = (bf16[1024,768]{1,0:T(8,128)(2,1)}, f32[1024,768]{1,0:T(8,128)}, bf16[4,2,4,24,768]{4,3,2,1,0:T(8,128)(2,1)}, f32[16,768]{1,0:T(8,128)}, bf16[...) custom-call(bf16[1024,768]{1,0:T(8,128)(2,1)} %bitcast.37, ...), custom_call_target="tpu_custom_call" | custom-call | flops 32614907904 | bytes 31457280 | tf_op jit(solution)/shard_map/middle_block/pallas_call | solution.py:1047
  136.4 92.5 %backward_block.1 = (f32[2,512,768]{2,1,0:T(8,128)}, f32[16,768]{1,0:T(8,128)}, bf16[3,2,4,32,768]{4,3,2,1,0:T(8,128)(2,1)}, bf16[2,4,24,3072]{3,2,1,0:T(8,128)(...) custom-call(bf16[2,9,1024,128]{3,2,1,0:T(8,128)(2,1)} %get-tuple-ele, ...), custom_call_target="tpu_custom_call", output_to_operand_aliasing={{2}: (14, {}), {3}: (15, {})} | custom-call | tf_op jit(solution)/shard_map/backward_block/pallas_call | solution.py:1339
  228.9 0.0 copy-start
  229.0 2.9 %bitcast_convert_fusion = f32[768,768]{1,0:T(8,128)} fusion(bf16[3,2,4,32,768]{4,3,2,1,0:T(8,128)(2,1)} %get-tuple-element.64), kind=kLoop, calls=%fused_computation | loop fusion | flops 589824 | bytes 3538944 | tf_op jit(solution)/shard_map/convert_element_type | solution.py:1497
  231.9 0.0 copy-done
  231.9 0.0 copy-start.3
  231.9 1.7 bitcast_convert_fusion.1
  233.6 0.0 copy-start.4
  233.6 0.0 copy-done.3
  233.7 0.0 copy-start.5
  233.7 0.0 copy-start.2
  233.7 1.4 bitcast_convert_fusion.2
  235.0 0.0 copy-done.4
  235.0 0.9 bitcast_convert_fusion.3
  235.9 0.0 copy-done.5
  235.9 0.7 fusion
  236.6 0.7 dynamic_slice.7
  237.3 0.0 copy-done.2
  237.3 0.0 copy-start.1
  237.3 1.1 copy.38
  238.4 1.3 copy-done.1
  239.7 1.7 copy.39
  (3 shorter events, 0.0 us)
Async XLA Ops:
  228.9 3.0 %copy-start = (bf16[2,4,24,3072]{3,2,1,0:T(8,128)(2,1)S(1)}, bf16[2,4,24,3072]{3,2,1,0:T(8,128)(2,1)}, u32[]{:S(2)}) copy-start(bf16[2,4,24,3072]{3,2,1,0:T(8,128)(2,1)} %get-tuple-element.63) | copy-start | bytes 3538948
  231.9 1.7 copy-start.3
  233.6 1.4 copy-start.4
  233.7 2.3 copy-start.5
  233.7 3.6 %copy-start.2 = (bf16[1024,768]{1,0:T(8,128)(2,1)S(1)}, bf16[1024,768]{1,0:T(8,128)(2,1)}, u32[]{:S(2)}) copy-start(bf16[1024,768]{1,0:T(8,128)(2,1)} %get-tuple-element.46) | copy-start | bytes 4718596
  237.3 2.5 %copy-start.1 = (f32[2,512,768]{2,1,0:T(8,128)S(1)}, f32[2,512,768]{2,1,0:T(8,128)}, u32[]{:S(2)}) copy-start(f32[2,512,768]{2,1,0:T(8,128)} %get-tuple-element.59) | copy-start | bytes 9437188
